TPU v7x, 128 devices: a whole 4x4x4 slice. The times are simulated.
128 devices in a mesh: lon: 32 (over y, z, core), lat: 4 (over x).
Axes of the slice: x: 4, y: 4, z: 4, core: 2. Of those that a mesh axis runs over, the one named last changes fastest.
Arguments:
- spectra: float32 [25, 36, 131072], P(None, None, ('lon', 'lat')), may hold values from 0 to 1
- wind_growth: float32 [131072], P(('lon', 'lat')), may hold values from 0.05 to 0.6
- wind_dir: float32 [131072], P(('lon', 'lat')), may hold values from -3.140625 to 3.140625
- point_cell: int32 [131072], P(('lon', 'lat')), may hold values from -1 to 131071, as said below
- land_mask: int32 [64, 2048], P('lon', 'lat'), may hold values from 0 to 1, as said below
- shoaling: float32 [64, 2048], P('lon', 'lat'), may hold values from 0.5 to 1
- slope_x: float32 [64, 2048], P('lon', 'lat'), may hold values from -0.5 to 0.5
- slope_y: float32 [64, 2048], P('lon', 'lat'), may hold values from -0.5 to 0.5
Outputs:
- wave_field: float32 [25, 36, 64, 2048], P(None, None, 'lon', 'lat')
Inputs may be any that keep to these rules, and one draw needn't show every extreme that they name: `point_cell`: every sea cell of land_mask is named by exactly one slot over all devices, land cells by none, other slots hold -1. The slots of one device name at most 8 cells of any one device's block of 2 x 512 cells, and in every draw some block gets exactly 8 from every device. `land_mask`: at least a quarter of the cells of each device's block are sea; some block is all sea.
All inputs are finite; a program needn't handle non-finite values.
Results may differ from a plain program's by a relative error of at most 0.0001.
Values sent between devices are 32-bit elements; how exact they have to be, the bound alone decides.
A program may use at most 128 MiB of HBM per device.

v0:
```python
import math

import jax
import jax.numpy as jnp
from jax import lax
from jax.sharding import PartitionSpec as P

NSUB = 2


def with_halo(cells, sides, width):
    for axis, dim in sides:
        count = lax.axis_size(axis)
        head = lax.slice_in_dim(cells, 0, width, axis=dim)
        tail = lax.slice_in_dim(cells, cells.shape[dim] - width, cells.shape[dim], axis=dim)
        cells = jnp.concatenate(
            [
                lax.ppermute(tail, axis, [(i, (i + 1) % count) for i in range(count)]),
                cells,
                lax.ppermute(head, axis, [((i + 1) % count, i) for i in range(count)]),
            ],
            axis=dim,
        )
    return cells


def spectral_tables(nfreq, ndir):
    level = jnp.arange(nfreq, dtype=jnp.float32)
    ratio = 1.1 ** (level - (nfreq - 1))
    speed = 0.65 * 1.1 ** (-level)
    width = 0.1 * 1.1**level
    theta = (jnp.arange(ndir, dtype=jnp.float32) + 0.5) * (2.0 * math.pi / ndir)
    return (ratio, speed, width, theta)


def route_rows(values, target, slots):
    picker = (target[:, None] == jnp.arange(slots, dtype=jnp.int32)[None, :]).astype(jnp.float32)
    return (
        jnp.dot(
            values, picker, precision=lax.Precision.HIGHEST, preferred_element_type=jnp.float32
        ),
        picker,
    )


def on_device(spectra, wind_growth, wind_dir, point_cell, land_mask, shoaling, slope_x, slope_y):
    nfreq, ndir, slots = spectra.shape
    rows_x, rows_y = land_mask.shape
    lon_count = lax.axis_size("lon")
    lat_count = lax.axis_size("lat")
    devices = lon_count * lat_count
    capacity = slots // devices
    ratio, speed, width, theta = spectral_tables(nfreq, ndir)
    dtheta = 2.0 * math.pi / ndir
    energy = jnp.sum((width * dtheta)[:, None] * jnp.sum(spectra, axis=1), axis=0)
    load = energy / (energy + 10.0)
    lobe = jnp.maximum(jnp.cos(theta[:, None] - wind_dir[None, :]), 0.0) ** 2
    rate = (
        wind_growth[None, None, :] * lobe[None] * ratio[:, None, None]
        - 0.4 * ratio[:, None, None] * load[None, None, :]
    )
    sourced = spectra * jnp.exp(rate)
    valid = point_cell >= 0
    cell = jnp.maximum(point_cell, 0)
    total_y = rows_y * lat_count
    col_x = cell // total_y
    col_y = cell % total_y
    owner = col_x // rows_x * lat_count + col_y // rows_y
    local = col_x % rows_x * rows_y + col_y % rows_y
    owner = jnp.where(valid, owner, devices)
    onehot = (owner[:, None] == jnp.arange(devices, dtype=jnp.int32)[None, :]).astype(jnp.int32)
    before = jnp.cumsum(onehot, axis=0) - onehot
    place = jnp.sum(before * onehot, axis=1)
    target = jnp.where(valid, owner * capacity + place, slots)
    outgoing, picker = route_rows(sourced.reshape(nfreq * ndir, slots), target, slots)
    outgoing = outgoing.reshape(nfreq, ndir, slots)
    filled = jnp.sum(picker, axis=0)
    labels = jnp.dot(
        local.astype(jnp.float32)[None, :],
        picker,
        precision=lax.Precision.HIGHEST,
        preferred_element_type=jnp.float32,
    )[0] - (1.0 - filled)
    rows_in, ids_in = (
        lax.all_to_all(outgoing, ("lon", "lat"), split_axis=2, concat_axis=2, tiled=True),
        lax.all_to_all(
            labels.reshape(1, 1, slots), ("lon", "lat"), split_axis=2, concat_axis=2, tiled=True
        ),
    )
    ids_in = ids_in.reshape(slots)
    placed = ids_in.astype(jnp.int32)
    placed = jnp.where(placed >= 0, placed, slots)
    field, unused = route_rows(rows_in.reshape(nfreq * ndir, slots), placed, slots)
    field = field.reshape(nfreq, ndir, rows_x, rows_y)
    sea = land_mask.astype(jnp.float32)
    cos_t = jnp.cos(theta)
    sin_t = jnp.sin(theta)
    speed4 = speed[:, None, None, None]
    cos4 = cos_t[None, :, None, None]
    sin4 = sin_t[None, :, None, None]
    shoal_pad = with_halo(shoaling, (("lon", 0), ("lat", 1)), 1)
    cx_pad = speed4 * shoal_pad[None, None] * cos4
    cy_pad = speed4 * shoal_pad[None, None] * sin4
    turn = speed4 * (sin4 * slope_x[None, None] - cos4 * slope_y[None, None])
    lat_id = lax.axis_index("lat")
    low_keep = (lat_id > 0).astype(jnp.float32)
    high_keep = (lat_id < lat_count - 1).astype(jnp.float32)
    edge = jnp.concatenate([low_keep[None], jnp.ones((rows_y,), jnp.float32), high_keep[None]])
    for step in range(NSUB):
        padded = with_halo(field, (("lon", 2), ("lat", 3)), 1) * edge
        qx = cx_pad * padded
        qy = cy_pad * padded
        flux_x = jnp.maximum(qx[:, :, :-1, 1:-1], 0.0) + jnp.minimum(qx[:, :, 1:, 1:-1], 0.0)
        flux_y = jnp.maximum(qy[:, :, 1:-1, :-1], 0.0) + jnp.minimum(qy[:, :, 1:-1, 1:], 0.0)
        half = (
            field
            - (flux_x[:, :, 1:] - flux_x[:, :, :-1])
            - (flux_y[:, :, :, 1:] - flux_y[:, :, :, :-1])
        )
        qt = turn * half
        flux_t = jnp.maximum(qt, 0.0) + jnp.minimum(jnp.roll(qt, -1, axis=1), 0.0)
        field = (half - flux_t + jnp.roll(flux_t, 1, axis=1)) * sea
    return field


def solution(mesh):
    placed = (
        P(None, None, ("lon", "lat")),
        P(("lon", "lat")),
        P(("lon", "lat")),
        P(("lon", "lat")),
        P("lon", "lat"),
        P("lon", "lat"),
        P("lon", "lat"),
        P("lon", "lat"),
    )
    return jax.shard_map(
        on_device,
        mesh=mesh,
        in_specs=placed,
        out_specs=P(None, None, "lon", "lat"),
        check_vma=False,
    )
```

profile of v0, /device:TPU:0, one launch (start us, length us, event | category | flops | bytes accessed | tf_op | source)
XLA Modules:
  0.0 387.0 jit_solution(16492591110037508928)
XLA Ops:
  5.3 11.4 %all-to-all-start.1 = ((f32[1,1,1024]{1,0,2:T(1,128)}), f32[1,1,1024]{1,0,2:T(1,128)S(1)}, u32[]{:S(2)}, u32[]{:S(2)}) async-start(f32[1,1,1024]{1,0,2:T(1,128)} %copy.59), calls=%async_computation.1 | async-start | bytes 1048576 | tf_op jit(solution)/shard_map/all_to_all | solution.py:86
  20.4 11.3 %fusion.8 = f32[25,36,1024]{2,1,0:T(8,128)} fusion(f32[25,36,1024]{2,1,0:T(8,128)} %param.8, s32[1024]{0:T(1024)S(1)} %add_select_fusion.6, f32[25,1024]{1,0:T(8,128)S(1)} %broadcast_multiply_fusion.1, f32[25]{0:T(128)S(1)} %add_power_fusion, f32[36,1024]{1,0:T(8,128)S(1)} %multiply_multiply_fusion.6), kind=kOutput, calls=%fused_computation.26 | convolution fusion | flops 11328434176 | bytes 7626852 | tf_op jit(solution)/shard_map/dot_general | solution.py:39
  31.7 14.6 %copy.58 = f32[25,36,1024]{1,0,2:T(8,128)} copy(f32[25,36,1024]{2,1,0:T(8,128)} %fusion.8) | data formatting | bytes 7372800 | tf_op jit(solution)/shard_map/dot_general | solution.py:39
  46.4 15.5 %reshape.196 = f32[128,1,7200]{2,1,0:T(1,128)} reshape(f32[1024,25,36]{2,1,0:T(8,128)} %bitcast.30) | data formatting | bytes 7372800
  61.9 10.8 %all-to-all-start = ((f32[128,1,7200]{2,1,0:T(1,128)}), f32[128,1,7200]{2,1,0:T(1,128)}, u32[]{:S(2)}, u32[]{:S(2)}) async-start(f32[128,1,7200]{2,1,0:T(1,128)} %reshape.196), calls=%async_computation | async-start | bytes 7471104 | tf_op jit(solution)/shard_map/all_to_all | solution.py:85
  72.7 18.3 %convert_reduce_fusion.1 = s32[1024]{0:T(1024)S(1)} fusion(f32[1,1,1024]{1,0,2:T(1,128)S(1)} %all-to-all-done.1), kind=kLoop, calls=%fused_computation.65 | loop fusion | flops 1024 | bytes 8192 | tf_op jit(solution)/shard_map/convert_element_type | solution.py:91
  91.0 28.5 %all-to-all-done = f32[128,1,7200]{2,1,0:T(1,128)} async-done(((f32[128,1,7200]{2,1,0:T(1,128)}), f32[128,1,7200]{2,1,0:T(1,128)}, u32[]{:S(2)}, u32[]{:S(2)}) %all-to-all-start) | async-done | bytes 3686432 | tf_op jit(solution)/shard_map/all_to_all | solution.py:85
  119.9 12.8 %reduce.2 = f32[128,7200]{1,0:T(8,128)} reduce(f32[128,1,7200]{2,1,0:T(1,128)} %all-to-all-done, f32[]{:T(128)} %broadcast.282), dimensions={1}, to_apply=%all_to_all.6.reduce_sub_computation | reduce | bytes 7372804 | tf_op jit(solution)/shard_map/all_to_all | solution.py:85
  132.7 12.2 %reshape.197 = f32[1024,25,36]{2,1,0:T(8,128)} reshape(f32[128,7200]{1,0:T(8,128)} %reduce.2) | data formatting | bytes 7372800
  145.0 11.6 %bitcast_bitcast_fusion = f32[25,36,1024,1]{1,0,2,3:T(8,128)} fusion(f32[1024,25,36]{2,1,0:T(8,128)} %reshape.197), kind=kLoop, calls=%fused_computation.126 | loop fusion | bytes 7372800 | tf_op jit(solution)/shard_map/all_to_all | solution.py:85
  156.6 52.4 %fusion = f32[25,36,2,512]{3,1,2,0:T(8,128)S(1)} fusion(f32[25,36,1024,1]{1,0,2,3:T(8,128)} %bitcast_bitcast_fusion, s32[2,512]{1,0:T(2,128)S(1)} %multiply_add_fusion, s32[1024]{0:T(1024)S(1)} %compare_select_fusion), kind=kOutput, calls=%fused_computation.4 | convolution fusion | flops 11325669376 | bytes 7380992 | tf_op jit(solution)/shard_map/dot_general | solution.py:39
  218.2 3.7 collective-permute-start.1
  222.8 20.2 %collective-permute-done = f32[1,512]{1,0:T(1,128)S(1)} collective-permute-done((f32[1,512]{1,0:T(1,128)S(1)}, f32[1,512]{1,0:T(1,128)S(1)}, u32[]{:S(2)}, u32[]{:S(2)}) %collective-permute-start) | collective-permute-done | bytes 2080 | tf_op jit(solution)/shard_map/ppermute | solution.py:18
  262.5 5.2 %collective-permute-done.6 = f32[25,36,4,1]{1,2,3,0:T(4,128)S(1)} collective-permute-done((f32[25,36,4,1]{1,2,3,0:T(4,128)S(1)}, f32[25,36,4,1]{1,2,3,0:T(4,128)S(1)}, u32[]{:S(2)}, u32[]{:S(2)}) %collective-permute-start.6) | collective-permute-done | bytes 14432 | tf_op jit(solution)/shard_map/ppermute | solution.py:18
  272.0 11.4 %multiply_multiply_fusion.3 = (f32[25,36,4,514]{3,1,2,0:T(8,128)S(1)}, f32[25,36,4,514]{3,1,2,0:T(8,128)}) fusion(f32[36]{0:T(128)S(1)} %get-tuple-element.28, f32[25,4,514]{2,1,0:T(4,128)S(1)} %broadcast_multiply_fusion, f32[514]{0:T(1024)S(1)} %pad_maximum_fusion.7, f32[25,36,4,1]{3,1,2,0:T(8,128)} %copy.68, f32[25,36,1,512]{3,1,2,0:T(8,128)S(1)} %copy.64, ...), kind=kLoop, calls=%fused_computation.3 | loop fusion | flops 16653600 | bytes 22412744 | tf_op jit(solution)/shard_map/mul | solution.py:111
  283.4 5.8 %fusion.3 = f32[25,36,3,512]{3,1,2,0:T(8,128)} fusion(f32[25,36,4,514]{3,1,2,0:T(8,128)S(1)} %get-tuple-element.11), kind=kLoop, calls=%fused_computation.12 | loop fusion | flops 4147200 | bytes 16588800 | tf_op jit(solution)/shard_map/add | solution.py:113
  289.2 5.5 %fusion.5 = f32[25,36,2,513]{3,1,2,0:T(8,128)S(1)} fusion(f32[25,36,4,514]{3,1,2,0:T(8,128)} %get-tuple-element.12), kind=kLoop, calls=%fused_computation.20 | loop fusion | flops 2770200 | bytes 11080800 | tf_op jit(solution)/shard_map/add | solution.py:114
  307.7 18.4 %collective-permute-done.9 = f32[25,36,1,512]{3,2,1,0:T(1,128)S(1)} collective-permute-done((f32[25,36,1,512]{3,2,1,0:T(1,128)S(1)}, f32[25,36,1,512]{3,2,1,0:T(1,128)S(1)}, u32[]{:S(2)}, u32[]{:S(2)}) %collective-permute-start.9) | collective-permute-done | bytes 1843232 | tf_op jit(solution)/shard_map/ppermute | solution.py:20
  326.3 7.0 %collective-permute-done.8 = f32[25,36,1,512]{3,2,1,0:T(1,128)S(1)} collective-permute-done((f32[25,36,1,512]{3,2,1,0:T(1,128)S(1)}, f32[25,36,1,512]{3,2,1,0:T(1,128)S(1)}, u32[]{:S(2)}, u32[]{:S(2)}) %collective-permute-start.8) | collective-permute-done | bytes 1843232 | tf_op jit(solution)/shard_map/ppermute | solution.py:18
  349.0 11.3 %multiply_multiply_fusion.2 = (f32[25,36,4,514]{3,1,2,0:T(8,128)S(1)}, f32[25,36,4,514]{3,1,2,0:T(8,128)}) fusion(f32[36]{0:T(128)S(1)} %get-tuple-element.28, f32[25,4,514]{2,1,0:T(4,128)S(1)} %copy-done.9, f32[514]{0:T(1024)S(1)} %pad_maximum_fusion.7, f32[25,36,4,1]{3,1,2,0:T(8,128)} %copy.76, f32[25,36,1,512]{3,1,2,0:T(8,128)S(1)} %copy.72, ...), kind=kLoop, calls=%fused_computation.2 | loop fusion | flops 16653600 | bytes 22412744 | tf_op jit(solution)/shard_map/mul | solution.py:111
  360.3 5.8 %fusion.2 = f32[25,36,3,512]{3,1,2,0:T(8,128)} fusion(f32[25,36,4,514]{3,1,2,0:T(8,128)S(1)} %get-tuple-element.9), kind=kLoop, calls=%fused_computation.9 | loop fusion | flops 4147200 | bytes 16588800 | tf_op jit(solution)/shard_map/add | solution.py:113
  366.1 5.5 %fusion.4 = f32[25,36,2,513]{3,1,2,0:T(8,128)S(1)} fusion(f32[25,36,4,514]{3,1,2,0:T(8,128)} %get-tuple-element.10), kind=kLoop, calls=%fused_computation.17 | loop fusion | flops 2770200 | bytes 11080800 | tf_op jit(solution)/shard_map/add | solution.py:114
  373.0 3.9 %multiply_multiply_fusion.4 = (f32[25,36,2,512]{3,1,2,0:T(8,128)S(1)}, f32[25,36,2,512]{3,1,2,0:T(8,128)}) fusion(f32[36,2,512]{2,0,1:T(8,128)S(1)} %copy-done.11, f32[25]{0:T(128)S(1)} %power_multiply_fusion, f32[25,36,2,513]{3,1,2,0:T(8,128)S(1)} %fusion.4, f32[25,36,2,512]{3,1,2,0:T(8,128)S(1)} %copy-done.4, f32[25,36,3,512]{3,1,2,0:T(8,128)S(1)} %bitcast.34), kind=kLoop, calls=%fused_computation.14 | loop fusion | flops 5529600 | bytes 25952356 | tf_op jit(solution)/shard_map/mul | solution.py:120
  381.8 4.7 %copy.77 = f32[25,36,2,512]{3,2,1,0:T(2,128)} copy(f32[25,36,2,512]{3,1,2,0:T(8,128)S(1)} %fusion.19) | data formatting | bytes 7372800 | tf_op jit(solution)/shard_map/mul | solution.py:122
  (133 shorter events, 78.0 us)
Async XLA Ops:
  1.2 18.5 %copy-start.13 = (f32[1024]{0:T(1024)S(1)}, f32[1024]{0:T(1024)}, u32[]{:S(2)}) copy-start(f32[1024]{0:T(1024)} %param.10) | copy-start | bytes 12292
  1.2 18.5 %copy-start.14 = (f32[1024]{0:T(1024)S(1)}, f32[1024]{0:T(1024)}, u32[]{:S(2)}) copy-start(f32[1024]{0:T(1024)} %param.9) | copy-start | bytes 12292
  5.3 56.6 %all-to-all-start.1 = ((f32[1,1,1024]{1,0,2:T(1,128)}), f32[1,1,1024]{1,0,2:T(1,128)S(1)}, u32[]{:S(2)}, u32[]{:S(2)}) async-start(f32[1,1,1024]{1,0,2:T(1,128)} %copy.59), calls=%async_computation.1 | async-start | bytes 1048576 | tf_op jit(solution)/shard_map/all_to_all | solution.py:86
  61.9 57.6 %all-to-all-start = ((f32[128,1,7200]{2,1,0:T(1,128)}), f32[128,1,7200]{2,1,0:T(1,128)}, u32[]{:S(2)}, u32[]{:S(2)}) async-start(f32[128,1,7200]{2,1,0:T(1,128)} %reshape.196), calls=%async_computation | async-start | bytes 7471104 | tf_op jit(solution)/shard_map/all_to_all | solution.py:85
  209.5 7.2 %copy-start.12 = (f32[2,512]{1,0:T(2,128)S(1)}, f32[2,512]{1,0:T(2,128)}, u32[]{:S(2)}) copy-start(f32[2,512]{1,0:T(2,128)} %param.13) | copy-start | bytes 12292
  209.5 12.6 %copy-start.15 = (f32[2,512]{1,0:T(2,128)S(1)}, f32[2,512]{1,0:T(2,128)}, u32[]{:S(2)}) copy-start(f32[2,512]{1,0:T(2,128)} %param.15) | copy-start | bytes 12292
  209.5 12.6 %copy-start.16 = (f32[2,512]{1,0:T(2,128)S(1)}, f32[2,512]{1,0:T(2,128)}, u32[]{:S(2)}) copy-start(f32[2,512]{1,0:T(2,128)} %param.14) | copy-start | bytes 12292
  209.5 13.3 %copy-start.17 = (s32[2,512]{1,0:T(2,128)S(1)}, s32[2,512]{1,0:T(2,128)}, u32[]{:S(2)}) copy-start(s32[2,512]{1,0:T(2,128)} %param.12) | copy-start | bytes 12292
  212.8 35.3 %collective-permute-start.5 = (f32[25,36,1,512]{3,2,1,0:T(1,128)S(1)}, f32[25,36,1,512]{3,2,1,0:T(1,128)}, u32[]{:S(2)}, u32[]{:S(2)}) collective-permute-start(f32[25,36,1,512]{3,2,1,0:T(1,128)S(1)} %copy.62), channel_id=1, source_target_pairs={{4,0},{8,4},{12,8},{16,12},{20,16},{24,20},{28,24},{32,28},{36,32}... | collective-permute-start | bytes 5529608 | tf_op jit(solution)/shard_map/ppermute | solution.py:20
  216.7 33.1 %collective-permute-start.4 = (f32[25,36,1,512]{3,2,1,0:T(1,128)}, f32[25,36,1,512]{3,2,1,0:T(1,128)}, u32[]{:S(2)}, u32[]{:S(2)}) collective-permute-start(f32[25,36,1,512]{3,2,1,0:T(1,128)} %copy.61), channel_id=1, source_target_pairs={{0,4},{4,8},{8,12},{12,16},{16,20},{20,24},{24,28},{28,32},{32,36}... | collective-permute-start | bytes 5529608 | tf_op jit(solution)/shard_map/ppermute | solution.py:18
  216.7 26.4 %collective-permute-start = (f32[1,512]{1,0:T(1,128)S(1)}, f32[1,512]{1,0:T(1,128)S(1)}, u32[]{:S(2)}, u32[]{:S(2)}) collective-permute-start(f32[1,512]{1,0:T(1,128)S(1)} %get-tuple-element.25), channel_id=1, source_target_pairs={{0,4},{4,8},{8,12},{12,16},{16,20},{20,24},{24,28},{28,32},{32,36}... | collective-permute-start | bytes 6152 | tf_op jit(solution)/shard_map/ppermute | solution.py:18
  218.2 24.9 %collective-permute-start.1 = (f32[1,512]{1,0:T(1,128)S(1)}, f32[1,512]{1,0:T(1,128)S(1)}, u32[]{:S(2)}, u32[]{:S(2)}) collective-permute-start(f32[1,512]{1,0:T(1,128)S(1)} %get-tuple-element.26), channel_id=1, source_target_pairs={{4,0},{8,4},{12,8},{16,12},{20,16},{24,20},{28,24},{32,28},{36,32}... | collective-permute-start | bytes 6152 | tf_op jit(solution)/shard_map/ppermute | solution.py:20
  221.9 29.6 %copy-start.1 = (f32[25,36,2,512]{3,1,2,0:T(8,128)S(1)}, f32[25,36,2,512]{3,1,2,0:T(8,128)}, u32[]{:S(2)}) copy-start(f32[25,36,2,512]{3,1,2,0:T(8,128)} %copy-done) | copy-start | bytes 11059204
  243.1 4.8 %collective-permute-start.2 = (f32[4,1]{1,0:T(4,128)S(1)}, f32[4,1]{1,0:T(4,128)S(1)}, u32[]{:S(2)}, u32[]{:S(2)}) collective-permute-start(f32[4,1]{1,0:T(4,128)S(1)} %get-tuple-element.21), channel_id=1, source_target_pairs={{0,1},{1,2},{2,3},{3,0},{4,5},{5,6},{6,7},{7,4},{8,9},{9,10},{10,1... | collective-permute-start | bytes 56 | tf_op jit(solution)/shard_map/ppermute | solution.py:18
  244.0 3.9 %collective-permute-start.3 = (f32[4,1]{1,0:T(4,128)S(1)}, f32[4,1]{1,0:T(4,128)S(1)}, u32[]{:S(2)}, u32[]{:S(2)}) collective-permute-start(f32[4,1]{1,0:T(4,128)S(1)} %get-tuple-element.22), channel_id=1, source_target_pairs={{1,0},{2,1},{3,2},{0,3},{5,4},{6,5},{7,6},{4,7},{9,8},{10,9},{11,1... | collective-permute-start | bytes 56 | tf_op jit(solution)/shard_map/ppermute | solution.py:20
  259.1 10.8 %collective-permute-start.7 = (f32[25,36,4,1]{1,2,3,0:T(4,128)S(1)}, f32[25,36,4,1]{1,2,3,0:T(4,128)S(1)}, u32[]{:S(2)}, u32[]{:S(2)}) collective-permute-start(f32[25,36,4,1]{1,2,3,0:T(4,128)S(1)} %copy.66), channel_id=1, source_target_pairs={{1,0},{2,1},{3,2},{0,3},{5,4},{6,5},{7,6},{4,7},{9,8},{10,9},{11,1... | collective-permute-start | bytes 43208 | tf_op jit(solution)/shard_map/ppermute | solution.py:20
  262.4 5.3 %collective-permute-start.6 = (f32[25,36,4,1]{1,2,3,0:T(4,128)S(1)}, f32[25,36,4,1]{1,2,3,0:T(4,128)S(1)}, u32[]{:S(2)}, u32[]{:S(2)}) collective-permute-start(f32[25,36,4,1]{1,2,3,0:T(4,128)S(1)} %copy.65), channel_id=1, source_target_pairs={{0,1},{1,2},{2,3},{3,0},{4,5},{5,6},{6,7},{7,4},{8,9},{9,10},{10,1... | collective-permute-start | bytes 43208 | tf_op jit(solution)/shard_map/ppermute | solution.py:18
  262.5 20.9 %copy-start.8 = (f32[25,4,514]{2,1,0:T(4,128)}, f32[25,4,514]{2,1,0:T(4,128)S(1)}, u32[]{:S(2)}) copy-start(f32[25,4,514]{2,1,0:T(4,128)S(1)} %broadcast_multiply_fusion) | copy-start | bytes 616804
  302.8 30.8 %copy-start.3 = (f32[25,36,2,512]{3,1,2,0:T(8,128)}, f32[25,36,2,512]{3,1,2,0:T(8,128)S(1)}, u32[]{:S(2)}) copy-start(f32[25,36,2,512]{3,1,2,0:T(8,128)S(1)} %fusion.17) | copy-start | bytes 11059204
  305.2 20.9 %collective-permute-start.9 = (f32[25,36,1,512]{3,2,1,0:T(1,128)S(1)}, f32[25,36,1,512]{3,2,1,0:T(1,128)S(1)}, u32[]{:S(2)}, u32[]{:S(2)}) collective-permute-start(f32[25,36,1,512]{3,2,1,0:T(1,128)S(1)} %copy.70), channel_id=1, source_target_pairs={{4,0},{8,4},{12,8},{16,12},{20,16},{24,20},{28,24},{32,28},{36,32}... | collective-permute-start | bytes 5529608 | tf_op jit(solution)/shard_map/ppermute | solution.py:20
  307.2 26.1 %collective-permute-start.8 = (f32[25,36,1,512]{3,2,1,0:T(1,128)S(1)}, f32[25,36,1,512]{3,2,1,0:T(1,128)S(1)}, u32[]{:S(2)}, u32[]{:S(2)}) collective-permute-start(f32[25,36,1,512]{3,2,1,0:T(1,128)S(1)} %copy.69), channel_id=1, source_target_pairs={{0,4},{4,8},{8,12},{12,16},{16,20},{20,24},{24,28},{28,32},{32,36}... | collective-permute-start | bytes 5529608 | tf_op jit(solution)/shard_map/ppermute | solution.py:18
  336.3 12.7 %copy-start.9 = (f32[25,4,514]{2,1,0:T(4,128)S(1)}, f32[25,4,514]{2,1,0:T(4,128)}, u32[]{:S(2)}) copy-start(f32[25,4,514]{2,1,0:T(4,128)} %copy-done.8) | copy-start | bytes 616804
  338.7 6.0 %collective-permute-start.10 = (f32[25,36,4,1]{1,2,3,0:T(4,128)S(1)}, f32[25,36,4,1]{1,2,3,0:T(4,128)S(1)}, u32[]{:S(2)}, u32[]{:S(2)}) collective-permute-start(f32[25,36,4,1]{1,2,3,0:T(4,128)S(1)} %copy.73), channel_id=1, source_target_pairs={{0,1},{1,2},{2,3},{3,0},{4,5},{5,6},{6,7},{7,4},{8,9},{9,10},{10,1... | collective-permute-start | bytes 43208 | tf_op jit(solution)/shard_map/ppermute | solution.py:18
  341.2 5.7 %collective-permute-start.11 = (f32[25,36,4,1]{1,2,3,0:T(4,128)S(1)}, f32[25,36,4,1]{1,2,3,0:T(4,128)S(1)}, u32[]{:S(2)}, u32[]{:S(2)}) collective-permute-start(f32[25,36,4,1]{1,2,3,0:T(4,128)S(1)} %copy.74), channel_id=1, source_target_pairs={{1,0},{2,1},{3,2},{0,3},{5,4},{6,5},{7,6},{4,7},{9,8},{10,9},{11,1... | collective-permute-start | bytes 43208 | tf_op jit(solution)/shard_map/ppermute | solution.py:20
  (12 other events, 61.4 us)
where the time goes:
time: 391 us; the launch traced here: 387 us
  other arithmetic  102 us (26%)
  local copies, waits for them, and re-layouts  99 us (25%)
  waiting for transfers between devices  80.8 us (21%)
  matrix products  65.2 us (17%)
  starting transfers between devices  39 us (10%)
    dot_general x2, matrix products, route_rows(): jnp.dot(values, picker, precision=lax.Precision.HIGHEST, preferred_elemen...  63.7 us
    ppermute x6, waiting for transfers between devices, with_halo(): lax.ppermute(tail, axis, [(i, (i + 1) % count) for i in range(count)])  34 us
    unnamed x46, local copies, waits for them, and re-layouts  33 us
    all_to_all x1, waiting for transfers between devices, on_device(): lax.all_to_all(outgoing, ('lon', 'lat'), split_axis=2, concat_axis=2, til...  28.5 us
    mul x2, other arithmetic, on_device(): qx = cx_pad * padded  22.7 us
    ppermute x6, waiting for transfers between devices, with_halo(): lax.ppermute(head, axis, [((i + 1) % count, i) for i in range(count)])  18.4 us
    convert_element_type x1, other arithmetic, on_device(): placed = ids_in.astype(jnp.int32)  18.3 us
    dot_general x1, local copies, waits for them, and re-layouts, route_rows(): jnp.dot(values, picker, precision=lax.Precision.HIGHEST, preferred_elemen...  14.6 us
  transfers between devices with their start and end apart: 14, of which 6 were waited for; matrix products, arithmetic and copies ran while one was open for 20% of the time, Pallas kernels for 0%

commit v1 on v0

v1 whole, which is shorter than its diff:
```python
import math

import jax
import jax.numpy as jnp
from jax import lax
from jax.experimental import pallas as pl
from jax.experimental.pallas import tpu as pltpu
from jax.sharding import PartitionSpec as P

MESH = pl.DeviceIdType.MESH
F32 = jnp.float32
BF16 = jnp.bfloat16

NF, ND = 25, 36
GX, GY = 2, 512
NLON, NLAT = 32, 4
NDEV = NLON * NLAT
CELLS = GX * GY
CAP = CELLS // NDEV
NT = 7
ROWS = 57
DTH = 2.0 * math.pi / ND
THETA = [(d + 0.5) * DTH for d in range(ND)]
COS = [math.cos(t) for t in THETA]
SIN = [math.sin(t) for t in THETA]
RATIO = [1.1 ** (f - (NF - 1)) for f in range(NF)]
WIDTH = [0.1 * 1.1**f * DTH for f in range(NF)]
CPLUS = [d for d in range(27, 36)] + [d for d in range(0, 9)]
CMINUS = [d for d in range(9, 27)]
SPLUS = list(range(0, 18))
SMINUS = list(range(18, 36))
PHALF = 9
VMEM_LIMIT = 60 << 20


def row_of(f, d):
    if f == NF - 1:
        return 36 * (NF - 1) + d
    base = 72 * (f // 2)
    if d < 32:
        return base + 32 * (f % 2) + d
    return base + 64 + 4 * (f % 2) + (d - 32)


def split(v):
    hi = v.astype(BF16)
    lo = (v - hi.astype(F32)).astype(BF16)
    return hi, lo


def nt_dot(a, b):
    return lax.dot_general(a, b, (((1,), (1,)), ((), ())), preferred_element_type=F32)


def nn_dot(a, b):
    return lax.dot_general(a, b, (((1,), (0,)), ((), ())), preferred_element_type=F32)


def source_kernel(spec_ref, wg_ref, wd_ref, pc_ref, out_ref, r_ref, v_ref, oh_ref, b_ref):
    wide = (1, CELLS)
    acc = jnp.zeros((8, CELLS), F32)
    acc4 = jnp.zeros((4, CELLS), F32)
    for f in range(NF):
        s = spec_ref[f, 0:8, :] + spec_ref[f, 8:16, :] + spec_ref[f, 16:24, :] + spec_ref[f, 24:32, :]
        acc = acc + WIDTH[f] * s
        acc4 = acc4 + WIDTH[f] * spec_ref[f, 32:36, :]
    energy = jnp.sum(acc, axis=0, keepdims=True) + jnp.sum(acc4, axis=0, keepdims=True)
    load = 0.4 * (energy / (energy + 10.0))
    wd = wd_ref[...]
    cw, sw = jnp.cos(wd), jnp.sin(wd)
    wg = wg_ref[...]
    for d in range(ND):
        lobe = jnp.maximum(COS[d] * cw + SIN[d] * sw, 0.0)
        r_ref[d : d + 1, :] = wg * (lobe * lobe) - load
    r32 = r_ref[0:32, :]
    r4 = r_ref[32:36, :]
    for f in range(0, NF, 2):
        base = 36 * f
        if f == NF - 1:
            v_ref[base : base + 32, :] = spec_ref[f, 0:32, :] * jnp.exp(RATIO[f] * r_ref[0:32, :])
            v_ref[base + 32 : base + 36, :] = spec_ref[f, 32:36, :] * jnp.exp(RATIO[f] * r_ref[32:36, :])
        else:
            g = f + 1
            v_ref[base : base + 32, :] = spec_ref[f, 0:32, :] * jnp.exp(RATIO[f] * r_ref[0:32, :])
            v_ref[base + 32 : base + 64, :] = spec_ref[g, 0:32, :] * jnp.exp(RATIO[g] * r_ref[0:32, :])
            v_ref[base + 64 : base + 68, :] = spec_ref[f, 32:36, :] * jnp.exp(RATIO[f] * r_ref[32:36, :])
            v_ref[base + 68 : base + 72, :] = spec_ref[g, 32:36, :] * jnp.exp(RATIO[g] * r_ref[32:36, :])

    pc = pc_ref[...]
    valid = pc >= 0
    cell = jnp.maximum(pc, 0)
    col_x = cell // (GY * NLAT)
    col_y = cell % (GY * NLAT)
    owner = (col_x // GX) * NLAT + col_y // GY
    local = (col_x % GX) * GY + col_y % GY
    owner = jnp.where(valid, owner, NDEV)
    own = (lax.broadcasted_iota(jnp.int32, (NDEV, CELLS), 0) == owner).astype(F32)
    own16 = own.astype(BF16)
    upper = (
        lax.broadcasted_iota(jnp.int32, (CELLS, CELLS), 0) < lax.broadcasted_iota(jnp.int32, (CELLS, CELLS), 1)
    ).astype(F32).astype(BF16)
    before = nn_dot(own16, upper)
    place = jnp.sum(before * own, axis=0, keepdims=True).astype(jnp.int32)
    target = jnp.where(valid, owner * CAP + place, CELLS)
    oh_ref[...] = (lax.broadcasted_iota(jnp.int32, (CELLS, CELLS), 0) == target).astype(F32).astype(BF16)

    b_ref[...] = jnp.zeros_like(b_ref)
    last = v_ref[128 * NT : 128 * NT + 4, :]
    ident = (local + 1).astype(F32)
    for s in range(CAP):
        here = (place == s).astype(F32)
        b_ref[4 * s : 4 * s + 4, :] = last * here
        b_ref[4 * CAP + s : 4 * CAP + s + 1, :] = ident * here
    bh, bl = split(b_ref[...])
    tail = nt_dot(own16, bh) + nt_dot(own16, bl)
    out_ref[:, 8 * NT, :] = tail

    def group(t, carry):
        hi, lo = split(v_ref[pl.ds(pl.multiple_of(128 * t, 128), 128), :])
        both = nt_dot(oh_ref[...], jnp.concatenate([hi, lo], axis=0))
        res = both[:, :128] + both[:, 128:]
        out_ref[:, pl.ds(pl.multiple_of(8 * t, 8), 8), :] = res.reshape(NDEV, CAP, 128)
        return carry

    lax.fori_loop(0, NT, group, 0)


def source(spectra, wg, wd, pc):
    return pl.pallas_call(
        source_kernel,
        out_shape=jax.ShapeDtypeStruct((NDEV, 64, 128), F32),
        in_specs=[pl.BlockSpec(memory_space=pltpu.VMEM)] * 4,
        out_specs=pl.BlockSpec(memory_space=pltpu.VMEM),
        scratch_shapes=[
            pltpu.VMEM((40, CELLS), F32),
            pltpu.VMEM((904, CELLS), F32),
            pltpu.VMEM((CELLS, CELLS), BF16),
            pltpu.VMEM((128, CELLS), F32),
        ],
        compiler_params=pltpu.CompilerParams(vmem_limit_bytes=VMEM_LIMIT),
        name="source",
    )(spectra, wg.reshape(1, CELLS), wd.reshape(1, CELLS), pc.reshape(1, CELLS))


def exchange_kernel(a_ref, o_ref, send_sem, recv_sem):
    lon = lax.axis_index("lon")
    x = lax.axis_index("lat")
    me = lon * NLAT + x
    c = lon % 2
    z = (lon // 2) % 4
    y = lon // 8

    def partner(r):
        dx = r % 4
        dy = (r // 4 + dx) % 4
        dz = (r // 16 + dx) % 4
        dc = r // 64
        return (((y + dy) % 4) * 4 + (z + dz) % 4) * 2 + (c + dc) % 2, (x + dx) % 4

    barrier = pltpu.get_barrier_semaphore()

    def greet(r, carry):
        pl.semaphore_signal(barrier, 1, device_id=partner(r), device_id_type=MESH)
        return carry

    lax.fori_loop(1, NDEV, greet, 0)
    pl.semaphore_wait(barrier, NDEV - 1)
    rows = pl.ds(0, ROWS)
    pltpu.make_async_copy(a_ref.at[me, rows], o_ref.at[me, rows], recv_sem).start()

    def push(r, carry):
        lo, la = partner(r)
        pltpu.make_async_remote_copy(
            src_ref=a_ref.at[lo * NLAT + la, rows],
            dst_ref=o_ref.at[me, rows],
            send_sem=send_sem,
            recv_sem=recv_sem,
            device_id=(lo, la),
            device_id_type=MESH,
        ).start()
        return carry

    lax.fori_loop(1, NDEV, push, 0)
    pltpu.make_async_copy(o_ref.at[:, rows], o_ref.at[:, rows], recv_sem).wait()
    sent = a_ref.at[pl.ds(0, NDEV - 1), rows]
    pltpu.make_async_copy(sent, sent, send_sem).wait()


def exchange(outgoing):
    return pl.pallas_call(
        exchange_kernel,
        out_shape=jax.ShapeDtypeStruct((NDEV, 64, 128), F32),
        in_specs=[pl.BlockSpec(memory_space=pltpu.VMEM)],
        out_specs=pl.BlockSpec(memory_space=pltpu.VMEM),
        scratch_shapes=[pltpu.SemaphoreType.DMA, pltpu.SemaphoreType.DMA],
        compiler_params=pltpu.CompilerParams(collective_id=0, has_side_effects=True, vmem_limit_bytes=VMEM_LIMIT),
        name="exchange",
    )(outgoing)


def as_tile(ref):
    return jnp.concatenate([ref[i : i + 1, 128 * j : 128 * (j + 1)] for i in range(GX) for j in range(4)], axis=0)


class Lattice:
    def __init__(self):
        sub = lax.broadcasted_iota(jnp.int32, (8, 128), 0)
        lane = lax.broadcasted_iota(jnp.int32, (8, 128), 1)
        self.lane = lane
        self.upper = sub >= 4
        self.lane0 = lane == 0
        self.lane127 = lane == 127
        self.first = (sub % 4 == 0) & self.lane0
        self.last = (sub % 4 == 3) & self.lane127
        self.lane0 = self.lane0 & (sub % 4 != 0)
        self.lane127 = self.lane127 & (sub % 4 != 3)


def lanes(v, k):
    return v if k % 128 == 0 else pltpu.roll(v, k % 128, 1)


def subs(v, k):
    return v if k % 8 == 0 else pltpu.roll(v, k % 8, 0)


def pack(lat, g, up_ref, dn_ref, yp_ref, ym_ref, f):
    for k in range(PHALF):
        up_ref[f, k] = jnp.where(lat.upper, g[CPLUS[k]], subs(g[CPLUS[k + PHALF]], 4))
        dn_ref[f, k] = jnp.where(lat.upper, subs(g[CMINUS[k + PHALF]], 4), g[CMINUS[k]])
    yp = jnp.zeros((8, 128), F32)
    ym = jnp.zeros((8, 128), F32)
    for k in range(18):
        yp = jnp.where(lat.lane == k, lanes(g[SPLUS[k]], k + 1), yp)
        ym = jnp.where(lat.lane == k, lanes(g[SMINUS[k]], k), ym)
    yp_ref[f] = yp
    ym_ref[f] = ym


def substep(lat, field, sh, sea, turns, speed, up, dn, yp, ym):
    yp = subs(yp, 5)
    ym = subs(ym, 3)
    half, pos, neg = [], [], []
    for d in range(ND):
        v = field(d)
        g = sh * v
        if d in CPLUS:
            k = CPLUS.index(d)
            if k < PHALF:
                gx = subs(jnp.where(lat.upper, up(k), g), 4)
            else:
                gx = jnp.where(lat.upper, subs(g, 4), up(k - PHALF))
        else:
            k = CMINUS.index(d)
            if k < PHALF:
                gx = subs(jnp.where(lat.upper, g, dn(k)), 4)
            else:
                gx = jnp.where(lat.upper, dn(k - PHALF), subs(g, 4))
        if d in SPLUS:
            k = SPLUS.index(d)
            r = lanes(g, 1)
            gy = jnp.where(lat.lane0, subs(r, 1), r)
            gy = jnp.where(lat.first, lanes(yp, -k), gy)
        else:
            k = SMINUS.index(d)
            r = lanes(g, 127)
            gy = jnp.where(lat.lane127, subs(r, 7), r)
            gy = jnp.where(lat.last, lanes(ym, 127 - k), gy)
        h = v - (speed * abs(COS[d])) * (g - gx) - (speed * abs(SIN[d])) * (g - gy)
        qt = (speed * turns(d)) * h
        half.append(h)
        pos.append(jnp.maximum(qt, 0.0))
        neg.append(jnp.minimum(qt, 0.0))
    new = []
    for d in range(ND):
        e, w = (d + 1) % ND, (d - 1) % ND
        new.append((half[d] - (pos[d] + neg[e]) + (pos[w] + neg[d])) * sea)
    return new


def fill_turns(turn_ref, sx_ref, sy_ref):
    sx, sy = as_tile(sx_ref), as_tile(sy_ref)
    for d in range(ND):
        turn_ref[d] = SIN[d] * sx - COS[d] * sy


def place_kernel(
    in_ref, mask_ref, sh_ref, sx_ref, sy_ref,
    f1_ref, up_in, dn_in, yp_in, ym_in,
    oh_ref, field_ref, turn_ref, up_out, dn_out, yp_out, ym_out, up2, dn2, yp2, ym2, up1, dn1, yp1, ym1,
    send_sem, recv_sem,
):
    lon = lax.axis_index("lon")
    x = lax.axis_index("lat")
    nxt = (lax.rem(lon + 1, NLON), x)
    prv = (lax.rem(lon + NLON - 1, NLON), x)
    ynxt = (lon, lax.rem(x + 1, NLAT))
    yprv = (lon, lax.rem(x + NLAT - 1, NLAT))
    barrier = pltpu.get_barrier_semaphore()
    for who in (nxt, prv, ynxt, yprv):
        pl.semaphore_signal(barrier, 1, device_id=who, device_id_type=MESH)

    sh = as_tile(sh_ref)
    sea = as_tile(mask_ref).astype(F32)
    fill_turns(turn_ref, sx_ref, sy_ref)
    lat = Lattice()

    tail = in_ref[:, 8 * NT, :]
    ident = tail[:, 4 * CAP : 5 * CAP]
    spread = (
        lax.broadcasted_iota(jnp.int32, (CAP, CELLS), 1) % CAP == lax.broadcasted_iota(jnp.int32, (CAP, CELLS), 0)
    ).astype(F32).astype(BF16)
    ih, il = split(ident)
    wide = nn_dot(ih, spread) + nn_dot(il, spread)
    mine = lax.broadcasted_iota(jnp.int32, (NDEV, CELLS), 1) // CAP == lax.broadcasted_iota(jnp.int32, (NDEV, CELLS), 0)
    ids = jnp.sum(jnp.where(mine, wide, 0.0), axis=0, keepdims=True).astype(jnp.int32) - 1
    oh_ref[...] = (lax.broadcasted_iota(jnp.int32, (CELLS, CELLS), 0) == ids).astype(F32).astype(BF16)

    def unplace(t, carry):
        hi, lo = split(in_ref[:, pl.ds(pl.multiple_of(8 * t, 8), 8), :].reshape(CELLS, 128))
        both = nn_dot(oh_ref[...], jnp.concatenate([hi, lo], axis=1))
        res = both[:, :128] + both[:, 128:]
        for ct in range(8):
            field_ref[pl.ds(pl.multiple_of(128 * t, 128), 128), ct, :] = res[128 * ct : 128 * (ct + 1), :].T
        return carry

    lax.fori_loop(0, NT, unplace, 0)
    cols = []
    for c in range(4):
        pick = (
            lax.broadcasted_iota(jnp.int32, (128, CELLS), 0) == 4 * (lax.broadcasted_iota(jnp.int32, (128, CELLS), 1) % CAP) + c
        ).astype(F32).astype(BF16)
        th, tl = split(tail)
        w = nn_dot(th, pick) + nn_dot(tl, pick)
        cols.append(jnp.sum(jnp.where(mine, w, 0.0), axis=0, keepdims=True))
    ch, cl = split(jnp.concatenate(cols + [jnp.zeros((4, CELLS), F32)], axis=0))
    tailv = nt_dot(ch, oh_ref[...]) + nt_dot(cl, oh_ref[...])
    for ct in range(8):
        field_ref[128 * NT : 128 * NT + 8, ct, :] = tailv[:, 128 * ct : 128 * (ct + 1)]

    def pack_one(f, row):
        g = [sh * field_ref[row(d)] for d in range(ND)]
        pack(lat, g, up_out, dn_out, yp_out, ym_out, f)

    def pack_pair(q, carry):
        base = 72 * q
        pack_one(2 * q, lambda d: base + row_of(0, d))
        pack_one(2 * q + 1, lambda d: base + row_of(1, d))
        return carry

    lax.fori_loop(0, NF // 2, pack_pair, 0)
    pack_one(NF - 1, lambda d: row_of(NF - 1, d))
    pl.semaphore_wait(barrier, 4)

    def copies(outs, ins, which):
        res = []
        for n, (src, dst, who) in enumerate(zip(outs, ins, (nxt, prv, ynxt, yprv))):
            res.append(
                pltpu.make_async_remote_copy(
                    src_ref=src, dst_ref=dst, send_sem=send_sem.at[which, n], recv_sem=recv_sem.at[which, n],
                    device_id=who, device_id_type=MESH,
                )
            )
        return res

    first = copies((up_out, dn_out, yp_out, ym_out), (up1, dn1, yp1, ym1), 0)
    for cp in first:
        cp.start()
    for cp in first:
        cp.wait()

    low = (x > 0).astype(F32)
    high = (x < NLAT - 1).astype(F32)

    def one(f, speed, row):
        new = substep(
            lat, lambda d: field_ref[row(d)], sh, sea, lambda d: turn_ref[d], speed,
            lambda k: up1[f, k], lambda k: dn1[f, k], yp1[f] * low, ym1[f] * high,
        )
        for d in range(ND):
            f1_ref[f, d] = new[d]
        pack(lat, [sh * v for v in new], up2, dn2, yp2, ym2, f)

    def pair(q, speed):
        base = 72 * q
        one(2 * q, speed, lambda d: base + row_of(0, d))
        one(2 * q + 1, speed * (1.0 / 1.1), lambda d: base + row_of(1, d))
        return speed * (1.0 / 1.21)

    speed = lax.fori_loop(0, NF // 2, pair, jnp.float32(0.65))
    one(NF - 1, speed, lambda d: row_of(NF - 1, d))
    second = copies((up2, dn2, yp2, ym2), (up_in, dn_in, yp_in, ym_in), 1)
    for cp in second:
        cp.start()
    for cp in second:
        cp.wait()


def face_shapes():
    return [(NF, PHALF, 8, 128), (NF, PHALF, 8, 128), (NF, 8, 128), (NF, 8, 128)]


def place(incoming, mask, sh, sx, sy):
    faces = [pltpu.VMEM(s, F32) for s in face_shapes()]
    return pl.pallas_call(
        place_kernel,
        out_shape=[jax.ShapeDtypeStruct((NF, ND, 8, 128), F32)] + [jax.ShapeDtypeStruct(s, F32) for s in face_shapes()],
        in_specs=[pl.BlockSpec(memory_space=pltpu.VMEM)] * 5,
        out_specs=[pl.BlockSpec(memory_space=pltpu.VMEM)] * 5,
        scratch_shapes=[
            pltpu.VMEM((CELLS, CELLS), BF16),
            pltpu.VMEM((904, 8, 128), F32),
            pltpu.VMEM((ND, 8, 128), F32),
        ]
        + faces * 3
        + [pltpu.SemaphoreType.DMA((2, 4)), pltpu.SemaphoreType.DMA((2, 4))],
        compiler_params=pltpu.CompilerParams(collective_id=1, has_side_effects=True, vmem_limit_bytes=VMEM_LIMIT),
        name="place",
    )(incoming, mask, sh, sx, sy)


def finish_kernel(f1_ref, up_ref, dn_ref, yp_ref, ym_ref, edge_ref, mask_ref, sh_ref, sx_ref, sy_ref, out_ref, turn_ref):
    sh = as_tile(sh_ref)
    sea = as_tile(mask_ref).astype(F32)
    fill_turns(turn_ref, sx_ref, sy_ref)
    lat = Lattice()
    x = edge_ref[0]
    low = (x > 0).astype(F32)
    high = (x < NLAT - 1).astype(F32)

    def one(f, speed):
        new = substep(
            lat, lambda d: f1_ref[f, d], sh, sea, lambda d: turn_ref[d], speed,
            lambda k: up_ref[f, k], lambda k: dn_ref[f, k], yp_ref[f] * low, ym_ref[f] * high,
        )
        for d in range(ND):
            out_ref[f, d, pl.ds(0, 4, 2), :] = new[d][0:4, :]
            out_ref[f, d, pl.ds(1, 4, 2), :] = new[d][4:8, :]
        return speed * (1.0 / 1.1)

    lax.fori_loop(0, NF, one, jnp.float32(0.65))


def finish(f1, up, dn, yp, ym, mask, sh, sx, sy):
    edge = lax.axis_index("lat").astype(jnp.int32).reshape(1)
    return pl.pallas_call(
        finish_kernel,
        out_shape=jax.ShapeDtypeStruct((NF, ND, 8, 128), F32),
        in_specs=[pl.BlockSpec(memory_space=pltpu.VMEM)] * 5
        + [pl.BlockSpec(memory_space=pltpu.SMEM)]
        + [pl.BlockSpec(memory_space=pltpu.VMEM)] * 4,
        out_specs=pl.BlockSpec(memory_space=pltpu.VMEM),
        scratch_shapes=[pltpu.VMEM((ND, 8, 128), F32)],
        compiler_params=pltpu.CompilerParams(vmem_limit_bytes=VMEM_LIMIT),
        name="finish",
    )(f1, up, dn, yp, ym, edge, mask, sh, sx, sy)


def on_device(spectra, wind_growth, wind_dir, point_cell, land_mask, shoaling, slope_x, slope_y):
    outgoing = source(spectra, wind_growth, wind_dir, point_cell)
    incoming = exchange(outgoing)
    f1, up, dn, yp, ym = place(incoming, land_mask, shoaling, slope_x, slope_y)
    out = finish(f1, up, dn, yp, ym, land_mask, shoaling, slope_x, slope_y)
    out = out.reshape(NF, ND, 4, GX, 128)
    return jnp.transpose(out, (0, 1, 3, 2, 4)).reshape(NF, ND, GX, GY)


def solution(mesh):
    placed = (
        P(None, None, ("lon", "lat")),
        P(("lon", "lat")),
        P(("lon", "lat")),
        P(("lon", "lat")),
        P("lon", "lat"),
        P("lon", "lat"),
        P("lon", "lat"),
        P("lon", "lat"),
    )
    return jax.shard_map(
        on_device, mesh=mesh, in_specs=placed, out_specs=P(None, None, "lon", "lat"), check_vma=False
    )
```

time: 391 us -> 132 us (0.34); the launches traced: 387 us -> 132 us
  Pallas kernels: 0 us -> 132 us
  other arithmetic: 102 us -> 0 us
  local copies, waits for them, and re-layouts: 99 us -> 0 us
  waiting for transfers between devices: 80.8 us -> 0 us
  matrix products: 65.2 us -> 0 us
  starting transfers between devices: 39 us -> 0 us
    pallas_call x0 -> x4, Pallas kernels: none -> 132 us  [the longest x1 62.1 us: exchange(): pl.pallas_call(exchange_kernel, out_shape=jax.ShapeDtypeStruct((NDEV, 64,...]
    dot_general x3 -> x0, matrix products: 65.2 us -> none  [the longest x2 63.7 us: route_rows(): jnp.dot(values, picker, precision=lax.Precision.HIGHEST, preferred_elemen...]
    ppermute x12 -> x0, waiting for transfers between devices: 52.3 us -> none  [the longest x6 34 us: with_halo(): lax.ppermute(tail, axis, [(i, (i + 1) % count) for i in range(count)])]
    mul x13 -> x0, other arithmetic: 33.8 us -> none  [the longest x2 22.7 us: on_device(): qx = cx_pad * padded]
    unnamed x46 -> x0, local copies, waits for them, and re-layouts: 33 us -> none
    all_to_all x2 -> x0, waiting for transfers between devices: 28.5 us -> none  [the longest x1 28.5 us: on_device(): lax.all_to_all(outgoing, ('lon', 'lat'), split_axis=2, concat_axis=2, til...]
    add x6 -> x0, other arithmetic: 25.1 us -> none  [the longest x2 11.6 us: on_device(): jnp.maximum(qx[:, :, :-1, 1:-1], 0.0) + jnp.minimum(qx[:, :, 1:, 1:-1], 0.0)]
    all_to_all x2 -> x0, starting transfers between devices: 22.2 us -> none  [the longest x1 11.4 us: on_device(): lax.all_to_all(labels.reshape(1, 1, slots), ('lon', 'lat'), split_axis=2,...]
  transfers between devices with their start and end apart: 14 -> 0, of which waited for: 6 -> 0; matrix products, arithmetic and copies ran while one was open for 20% -> 0% of each run, Pallas kernels for 0% -> 0%
where the time goes in v1:
time: 132 us
  Pallas kernels  132 us (100%)
    pallas_call x1, Pallas kernels, exchange(): pl.pallas_call(exchange_kernel, out_shape=jax.ShapeDtypeStruct((NDEV, 64,...  62.1 us
    pallas_call x1, Pallas kernels, place(): pl.pallas_call(place_kernel, out_shape=[jax.ShapeDtypeStruct((NF, ND, 8,...  48.8 us
    pallas_call x1, Pallas kernels, source(): pl.pallas_call(source_kernel, out_shape=jax.ShapeDtypeStruct((NDEV, 64, 1...  12.2 us
    pallas_call x1, Pallas kernels, finish(): pl.pallas_call(finish_kernel, out_shape=jax.ShapeDtypeStruct((NF, ND, 8,...  8.77 us

profile of v1, /device:TPU:0, one launch (start us, length us, event | category | flops | bytes accessed | tf_op | source)
XLA Modules:
  0.0 131.9 jit_solution(6751034886309606465)
XLA Ops:
  0.0 12.2 %source.1.a_ref = f32[128,64,128]{2,1,0:T(8,128)} custom-call(f32[25,36,1024]{2,1,0:T(8,128)} %spec_ref.1, f32[1,1024]{1,0:T(1,128)} %bitcast.9, f32[1,1024]{1,0:T(1,128)} %bitcast.10, s32[1,1024]{1,0:T(1,128)} %bitcast.11), custom_call_target="tpu_custom_call" | custom-call | tf_op jit(solution)/shard_map/source/pallas_call | solution.py:129
  12.2 62.1 %exchange.1.in_ref = f32[128,64,128]{2,1,0:T(8,128)} custom-call(f32[128,64,128]{2,1,0:T(8,128)} %source.1.a_ref), custom_call_target="tpu_custom_call" | custom-call | tf_op jit(solution)/shard_map/exchange/pallas_call | solution.py:190
  74.3 48.8 %place.1 = (f32[25,36,8,128]{3,2,1,0:T(8,128)}, f32[25,9,8,128]{3,2,1,0:T(8,128)}, f32[25,9,8,128]{3,2,1,0:T(8,128)}, f32[25,8,128]{2,1,0:T(8,128)}, f32[25,8,128]{2,1,0:T(8,128)}) custom-call(f32[128,64,128]{2,1,0:T(8,128)} %exchange.1.in_ref, s32[2,512]{1,0:T(2,128)} %mask_ref.3, f32[2,512]{1,0:T(2,128)} %sh_ref.3, f32[2,512]{1,0:T(2,128)} %sx_ref.3, ...), custom_call_target="tpu_custom_call" | custom-call | tf_op jit(solution)/shard_map/place/pallas_call | solution.py:405
  123.2 8.8 %finish.1 = f32[25,36,8,128]{3,2,1,0:T(8,128)} custom-call(f32[25,36,8,128]{3,2,1,0:T(8,128)} %get-tuple-element.10.f1_ref, f32[25,9,8,128]{3,2,1,0:T(8,128)} %get-tuple-element.11.up_ref, f32[25,9,8,128]{3,2,1,0:T(8,128)} %get-tuple-element.12.dn_ref, f32[25,8,128]{2,1,0:T(8,128)} %get-tuple-element.13.yp_ref, f32[25,8,128]{2,1,0:T(8,128)} %get-tuple-element.14.ym_ref, ...), custom_call_target="tpu_custom_call" | custom-call | tf_op jit(solution)/shard_map/finish/pallas_call | solution.py:446

commit v2 on v0

v2 whole, which is shorter than its diff:
```python
import math

import jax
import jax.numpy as jnp
from jax import lax
from jax.experimental import pallas as pl
from jax.experimental.pallas import tpu as pltpu
from jax.sharding import PartitionSpec as P

MESH = pl.DeviceIdType.MESH
F32 = jnp.float32
BF16 = jnp.bfloat16

NF, ND = 25, 36
GX, GY = 2, 512
NLON, NLAT = 32, 4
NDEV = NLON * NLAT
CELLS = GX * GY
CAP = CELLS // NDEV
NT = 7
ROWS = 57
DTH = 2.0 * math.pi / ND
THETA = [(d + 0.5) * DTH for d in range(ND)]
COS = [math.cos(t) for t in THETA]
SIN = [math.sin(t) for t in THETA]
RATIO = [1.1 ** (f - (NF - 1)) for f in range(NF)]
WIDTH = [0.1 * 1.1**f * DTH for f in range(NF)]
CPLUS = [d for d in range(27, 36)] + [d for d in range(0, 9)]
CMINUS = [d for d in range(9, 27)]
SPLUS = list(range(0, 18))
SMINUS = list(range(18, 36))
PHALF = 9
VMEM_LIMIT = 60 << 20


def row_of(f, d):
    if f == NF - 1:
        return 36 * (NF - 1) + d
    base = 72 * (f // 2)
    if d < 32:
        return base + 32 * (f % 2) + d
    return base + 64 + 4 * (f % 2) + (d - 32)


def row_dyn(f, d):
    base = 72 * lax.div(f, 2)
    if d < 32:
        return base + 32 * lax.rem(f, 2) + d
    return base + jnp.where(f == NF - 1, 32, 64 + 4 * lax.rem(f, 2)) + (d - 32)


def whole(t):
    t = jnp.clip(t, 0, NT)
    return 2 * lax.div(16 * t, 9) + lax.div(t, NT)


def split(v):
    hi = v.astype(BF16)
    lo = (v - hi.astype(F32)).astype(BF16)
    return hi, lo


def nt_dot(a, b):
    return lax.dot_general(a, b, (((1,), (1,)), ((), ())), preferred_element_type=F32)


def nn_dot(a, b):
    return lax.dot_general(a, b, (((1,), (0,)), ((), ())), preferred_element_type=F32)


def as_tile(ref):
    return jnp.concatenate([ref[i : i + 1, 128 * j : 128 * (j + 1)] for i in range(GX) for j in range(4)], axis=0)


class Lattice:
    def __init__(self):
        sub = lax.broadcasted_iota(jnp.int32, (8, 128), 0)
        lane = lax.broadcasted_iota(jnp.int32, (8, 128), 1)
        self.lane = lane
        self.upper = sub >= 4
        self.lane0 = lane == 0
        self.lane127 = lane == 127
        self.first = (sub % 4 == 0) & self.lane0
        self.last = (sub % 4 == 3) & self.lane127
        self.lane0 = self.lane0 & (sub % 4 != 0)
        self.lane127 = self.lane127 & (sub % 4 != 3)


def lanes(v, k):
    return v if k % 128 == 0 else pltpu.roll(v, k % 128, 1)


def subs(v, k):
    return v if k % 8 == 0 else pltpu.roll(v, k % 8, 0)


def pack(lat, g, up_ref, dn_ref, yp_ref, ym_ref):
    for k in range(PHALF):
        up_ref[k] = jnp.where(lat.upper, g[CPLUS[k]], subs(g[CPLUS[k + PHALF]], 4))
        dn_ref[k] = jnp.where(lat.upper, subs(g[CMINUS[k + PHALF]], 4), g[CMINUS[k]])
    yp = jnp.zeros((8, 128), F32)
    ym = jnp.zeros((8, 128), F32)
    for k in range(18):
        yp = jnp.where(lat.lane == k, lanes(g[SPLUS[k]], k + 1), yp)
        ym = jnp.where(lat.lane == k, lanes(g[SMINUS[k]], k), ym)
    yp_ref[...] = yp
    ym_ref[...] = ym


def substep(lat, field, sh, sea, turns, speed, up, dn, yp, ym):
    yp = subs(yp, 5)
    ym = subs(ym, 3)
    half, pos, neg = [], [], []
    for d in range(ND):
        v = field(d)
        g = sh * v
        if d in CPLUS:
            k = CPLUS.index(d)
            if k < PHALF:
                gx = subs(jnp.where(lat.upper, up(k), g), 4)
            else:
                gx = jnp.where(lat.upper, subs(g, 4), up(k - PHALF))
        else:
            k = CMINUS.index(d)
            if k < PHALF:
                gx = subs(jnp.where(lat.upper, g, dn(k)), 4)
            else:
                gx = jnp.where(lat.upper, dn(k - PHALF), subs(g, 4))
        if d in SPLUS:
            k = SPLUS.index(d)
            r = lanes(g, 1)
            gy = jnp.where(lat.lane0, subs(r, 1), r)
            gy = jnp.where(lat.first, lanes(yp, -k), gy)
        else:
            k = SMINUS.index(d)
            r = lanes(g, 127)
            gy = jnp.where(lat.lane127, subs(r, 7), r)
            gy = jnp.where(lat.last, lanes(ym, 127 - k), gy)
        h = v - (speed * abs(COS[d])) * (g - gx) - (speed * abs(SIN[d])) * (g - gy)
        qt = (speed * turns(d)) * h
        half.append(h)
        pos.append(jnp.maximum(qt, 0.0))
        neg.append(jnp.minimum(qt, 0.0))
    new = []
    for d in range(ND):
        e, w = (d + 1) % ND, (d - 1) % ND
        new.append((half[d] - (pos[d] + neg[e]) + (pos[w] + neg[d])) * sea)
    return new


def fill_turns(turn_ref, sx_ref, sy_ref):
    sx, sy = as_tile(sx_ref), as_tile(sy_ref)
    for d in range(ND):
        turn_ref[d] = SIN[d] * sx - COS[d] * sy


def step_kernel(
    spec_hbm, wg_ref, wd_ref, pc_ref, mask_ref, sh_ref, sx_ref, sy_ref, out_hbm,
    spec_ref, r_ref, v_ref, b_ref, sbuf, rbuf, ohs_ref, ohr_ref, field_ref, f1_ref, stage_ref, turn_ref,
    up_out, dn_out, yp_out, ym_out, up_in, dn_in, yp_in, ym_in, table,
    spec_sem, send_sem, recv_sem, face_send, face_recv, out_sem,
):
    lon = lax.axis_index("lon")
    x = lax.axis_index("lat")
    me = lon * NLAT + x
    c = lax.rem(lon, 2)
    z = lax.rem(lax.div(lon, 2), 4)
    y = lax.div(lon, 8)
    nxt = (lax.rem(lon + 1, NLON), x)
    prv = (lax.rem(lon + NLON - 1, NLON), x)
    ynxt = (lon, lax.rem(x + 1, NLAT))
    yprv = (lon, lax.rem(x + NLAT - 1, NLAT))

    loads = [
        pltpu.make_async_copy(spec_hbm.at[pl.ds(5 * i, 5)], spec_ref.at[pl.ds(5 * i, 5)], spec_sem.at[i])
        for i in range(5)
    ]
    for cp in loads:
        cp.start()

    barrier = pltpu.get_barrier_semaphore()

    def greet(r, carry):
        who = lax.rem(me + r, NDEV)
        pl.semaphore_signal(barrier, 1, device_id=(lax.div(who, NLAT), lax.rem(who, NLAT)), device_id_type=MESH)
        return carry

    lax.fori_loop(1, NDEV, greet, 0)
    for f in range(NF):
        table[f] = jnp.float32(RATIO[f])
        table[32 + f] = jnp.float32(0.65 * 1.1 ** (-f))

    pc = pc_ref[...]
    valid = pc >= 0
    cell = jnp.maximum(pc, 0)
    col_x = cell // (GY * NLAT)
    col_y = cell % (GY * NLAT)
    owner = (col_x // GX) * NLAT + col_y // GY
    local = (col_x % GX) * GY + col_y % GY
    owner = jnp.where(valid, owner, NDEV)
    own = (lax.broadcasted_iota(jnp.int32, (NDEV, CELLS), 0) == owner).astype(F32)
    own16 = own.astype(BF16)
    ohs_ref[...] = (
        lax.broadcasted_iota(jnp.int32, (CELLS, CELLS), 0) < lax.broadcasted_iota(jnp.int32, (CELLS, CELLS), 1)
    ).astype(F32).astype(BF16)
    before = nn_dot(own16, ohs_ref[...])
    where = jnp.sum(before * own, axis=0, keepdims=True).astype(jnp.int32)
    target = jnp.where(valid, owner * CAP + where, CELLS)
    ohs_ref[...] = (lax.broadcasted_iota(jnp.int32, (CELLS, CELLS), 0) == target).astype(F32).astype(BF16)

    wd = wd_ref[...]
    cw, sw = jnp.cos(wd), jnp.sin(wd)
    wg = wg_ref[...]
    acc = jnp.zeros((8, CELLS), F32)
    acc4 = jnp.zeros((4, CELLS), F32)
    for f in range(NF):
        if f % 5 == 0:
            loads[f // 5].wait()
        s = spec_ref[f, 0:8, :] + spec_ref[f, 8:16, :] + spec_ref[f, 16:24, :] + spec_ref[f, 24:32, :]
        acc = acc + WIDTH[f] * s
        acc4 = acc4 + WIDTH[f] * spec_ref[f, 32:36, :]
    energy = jnp.sum(acc, axis=0, keepdims=True) + jnp.sum(acc4, axis=0, keepdims=True)
    load = 0.4 * (energy / (energy + 10.0))
    for d in range(ND):
        lobe = jnp.maximum(COS[d] * cw + SIN[d] * sw, 0.0)
        r_ref[d : d + 1, :] = wg * (lobe * lobe) - load

    last_base = 36 * (NF - 1)
    v_ref[last_base : last_base + 32, :] = spec_ref[NF - 1, 0:32, :] * jnp.exp(RATIO[NF - 1] * r_ref[0:32, :])
    v_ref[last_base + 32 : last_base + 36, :] = spec_ref[NF - 1, 32:36, :] * jnp.exp(RATIO[NF - 1] * r_ref[32:36, :])

    b_ref[...] = jnp.zeros_like(b_ref)
    last = v_ref[128 * NT : 128 * NT + 4, :]
    ident = (local + 1).astype(F32)
    for s in range(CAP):
        here = (where == s).astype(F32)
        b_ref[4 * s : 4 * s + 4, :] = last * here
        b_ref[4 * CAP + s : 4 * CAP + s + 1, :] = ident * here
    bh, bl = split(b_ref[...])
    sbuf[:, 8 * NT, :] = nt_dot(own16, bh) + nt_dot(own16, bl)

    def push(rows, sem):
        pltpu.make_async_copy(sbuf.at[me, rows], rbuf.at[me, rows], sem).start()

        def go(j, carry):
            b, e, dc = lax.rem(j, 4), lax.rem(lax.div(j, 4), 4), lax.div(j, 16)
            cc = lax.rem(c + dc, 2)
            for a in range(4):
                lo = (lax.rem(y + b + a, 4) * 4 + lax.rem(z + e + a, 4)) * 2 + cc
                la = lax.rem(x + a, 4)
                copy = pltpu.make_async_remote_copy(
                    src_ref=sbuf.at[lo * NLAT + la, rows], dst_ref=rbuf.at[me, rows],
                    send_sem=send_sem, recv_sem=sem, device_id=(lo, la), device_id_type=MESH,
                )
                if a == 0:
                    pl.when(j > 0)(copy.start)
                else:
                    copy.start()
            return carry

        lax.fori_loop(0, NDEV // 4, go, 0)

    def tile(t):
        return pl.ds(pl.multiple_of(8 * t, 8), 8)

    def arrive(rows, sem):
        pltpu.make_async_copy(rbuf.at[:, rows], rbuf.at[:, rows], sem).wait()

    def grow(q, carry):
        base = pl.multiple_of(72 * q, 8)
        f, g = 2 * q, 2 * q + 1
        e4 = []
        for i, h in enumerate((f, g)):
            ratio = table[h]
            v_ref[pl.ds(base + 32 * i, 32), :] = spec_ref[h, 0:32, :] * jnp.exp(ratio * r_ref[0:32, :])
            e4.append(spec_ref[h, 32:36, :] * jnp.exp(ratio * r_ref[32:36, :]))
        v_ref[pl.ds(base + 64, 8), :] = jnp.concatenate(e4, axis=0)
        return carry

    def pairs(t):
        return jnp.where(t == 0, 0, jnp.minimum(lax.div(16 * t + 8, 9), NF // 2))

    def group(t):
        lax.fori_loop(pairs(t), pairs(t + 1), grow, 0)
        hi, lo = split(v_ref[pl.ds(pl.multiple_of(128 * t, 128), 128), :])
        both = nt_dot(ohs_ref[...], jnp.concatenate([hi, lo], axis=0))
        res = both[:, :128] + both[:, 128:]
        sbuf[:, tile(t), :] = res.reshape(NDEV, CAP, 128)

    pl.semaphore_wait(barrier, NDEV - 1)
    push(pl.ds(8 * NT, 1), recv_sem.at[NT])

    def prologue(t, carry):
        group(t)

        @pl.when(t < 2)
        def _():
            push(tile(t), recv_sem.at[t])

        return carry

    lax.fori_loop(0, 3, prologue, 0)

    sh = as_tile(sh_ref)
    sea = as_tile(mask_ref).astype(F32)
    fill_turns(turn_ref, sx_ref, sy_ref)
    lat = Lattice()
    low = (x > 0).astype(F32)
    high = (x < NLAT - 1).astype(F32)

    arrive(pl.ds(8 * NT, 1), recv_sem.at[NT])
    tail = rbuf[:, 8 * NT, :]
    ident = tail[:, 4 * CAP : 5 * CAP]
    spread = (
        lax.broadcasted_iota(jnp.int32, (CAP, CELLS), 1) % CAP == lax.broadcasted_iota(jnp.int32, (CAP, CELLS), 0)
    ).astype(F32).astype(BF16)
    ih, il = split(ident)
    wide = nn_dot(ih, spread) + nn_dot(il, spread)
    mine = lax.broadcasted_iota(jnp.int32, (NDEV, CELLS), 1) // CAP == lax.broadcasted_iota(jnp.int32, (NDEV, CELLS), 0)
    ids = jnp.sum(jnp.where(mine, wide, 0.0), axis=0, keepdims=True).astype(jnp.int32) - 1
    ohr_ref[...] = (lax.broadcasted_iota(jnp.int32, (CELLS, CELLS), 0) == ids).astype(F32).astype(BF16)
    cols = []
    th, tl = split(tail)
    for k in range(4):
        pick = (
            lax.broadcasted_iota(jnp.int32, (128, CELLS), 0) == 4 * (lax.broadcasted_iota(jnp.int32, (128, CELLS), 1) % CAP) + k
        ).astype(F32).astype(BF16)
        w = nn_dot(th, pick) + nn_dot(tl, pick)
        cols.append(jnp.sum(jnp.where(mine, w, 0.0), axis=0, keepdims=True))
    ch, cl = split(jnp.concatenate(cols + [jnp.zeros((4, CELLS), F32)], axis=0))
    tailv = nt_dot(ch, ohr_ref[...]) + nt_dot(cl, ohr_ref[...])
    for ct in range(8):
        field_ref[128 * NT : 128 * NT + 8, ct, :] = tailv[:, 128 * ct : 128 * (ct + 1)]

    def unplace(t):
        hi, lo = split(rbuf[:, tile(t), :].reshape(CELLS, 128))
        both = nn_dot(ohr_ref[...], jnp.concatenate([hi, lo], axis=1))
        res = both[:, :128] + both[:, 128:]
        for ct in range(8):
            field_ref[pl.ds(pl.multiple_of(128 * t, 128), 128), ct, :] = res[128 * ct : 128 * (ct + 1), :].T

    def faces(s, f):
        bufs = zip((up_out, dn_out, yp_out, ym_out), (up_in, dn_in, yp_in, ym_in), (nxt, prv, ynxt, yprv))
        return [
            pltpu.make_async_remote_copy(
                src_ref=src.at[s, f], dst_ref=dst.at[s, f], send_sem=face_send.at[s, n],
                recv_sem=face_recv.at[s, n, f], device_id=who, device_id_type=MESH,
            )
            for n, (src, dst, who) in enumerate(bufs)
        ]

    def send(s, f):
        for copy in faces(s, f):
            copy.start()

    def await_faces(s, f):
        for copy in faces(s, f):
            copy.wait_recv()

    def wrap(s, f, g):
        pack(lat, g, up_out.at[s, f], dn_out.at[s, f], yp_out.at[s, f], ym_out.at[s, f])

    def propagate(s, f, get):
        await_faces(s, f)
        return substep(
            lat, get, sh, sea, lambda d: turn_ref[d], table[32 + f],
            lambda k: up_in[s, f, k], lambda k: dn_in[s, f, k], yp_in[s, f] * low, ym_in[s, f] * high,
        )

    def over(lo, hi, fn):
        def body(f, carry):
            fn(f)
            return carry

        lax.fori_loop(lo, hi, body, 0)

    def start_face(f):
        wrap(0, f, [sh * field_ref[row_dyn(f, d)] for d in range(ND)])

    def first(f):
        new = propagate(0, f, lambda d: field_ref[row_dyn(f, d)])
        for d in range(ND):
            f1_ref[f, d] = new[d]
        wrap(1, f, [sh * v for v in new])

    def second(f):
        new = propagate(1, f, lambda d: f1_ref[f, d])
        for d in range(ND):
            stage_ref[f, d, pl.ds(0, 4, 2), :] = new[d][0:4, :]
            stage_ref[f, d, pl.ds(1, 4, 2), :] = new[d][4:8, :]

    def emit(f):
        pltpu.make_async_copy(stage_ref.at[f], out_hbm.at[f], out_sem).start()

    def step(t, carry):
        @pl.when(t < NT)
        def _():
            arrive(tile(t), recv_sem.at[t])
            unplace(t)

        over(whole(t), whole(t + 1), start_face)
        over(whole(t), whole(t + 1), lambda f: send(0, f))

        @pl.when(t + 2 < NT)
        def _():
            push(tile(t + 2), recv_sem.at[t + 2])

        @pl.when(t + 3 < NT)
        def _():
            group(t + 3)

        over(whole(t - 1), whole(t), first)
        over(whole(t - 1), whole(t), lambda f: send(1, f))
        over(whole(t - 2), whole(t - 1), second)
        over(whole(t - 2), whole(t - 1), emit)
        return carry

    lax.fori_loop(0, NT + 2, step, 0)
    sent = sbuf.at[pl.ds(0, NDEV - 1), pl.ds(0, ROWS)]
    pltpu.make_async_copy(sent, sent, send_sem).wait()
    for s in range(2):
        for n, src in enumerate((up_out, dn_out, yp_out, ym_out)):
            pltpu.make_async_copy(src.at[s], src.at[s], face_send.at[s, n]).wait()
    pltpu.make_async_copy(stage_ref, out_hbm, out_sem).wait()


def on_device(spectra, wind_growth, wind_dir, point_cell, land_mask, shoaling, slope_x, slope_y):
    face = [(2, NF, PHALF, 8, 128), (2, NF, PHALF, 8, 128), (2, NF, 8, 128), (2, NF, 8, 128)]
    out = pl.pallas_call(
        step_kernel,
        out_shape=jax.ShapeDtypeStruct((NF, ND, 8, 128), F32),
        in_specs=[pl.BlockSpec(memory_space=pl.ANY)] + [pl.BlockSpec(memory_space=pltpu.VMEM)] * 7,
        out_specs=pl.BlockSpec(memory_space=pl.ANY),
        scratch_shapes=[
            pltpu.VMEM((NF, ND, CELLS), F32),
            pltpu.VMEM((40, CELLS), F32),
            pltpu.VMEM((904, CELLS), F32),
            pltpu.VMEM((128, CELLS), F32),
            pltpu.VMEM((NDEV, 64, 128), F32),
            pltpu.VMEM((NDEV, 64, 128), F32),
            pltpu.VMEM((CELLS, CELLS), BF16),
            pltpu.VMEM((CELLS, CELLS), BF16),
            pltpu.VMEM((904, 8, 128), F32),
            pltpu.VMEM((NF, ND, 8, 128), F32),
            pltpu.VMEM((NF, ND, 8, 128), F32),
            pltpu.VMEM((ND, 8, 128), F32),
        ]
        + [pltpu.VMEM(s, F32) for s in face] * 2
        + [
            pltpu.SMEM((64,), F32),
            pltpu.SemaphoreType.DMA((5,)),
            pltpu.SemaphoreType.DMA,
            pltpu.SemaphoreType.DMA((NT + 1,)),
            pltpu.SemaphoreType.DMA((2, 4)),
            pltpu.SemaphoreType.DMA((2, 4, NF)),
            pltpu.SemaphoreType.DMA,
        ],
        compiler_params=pltpu.CompilerParams(collective_id=0, has_side_effects=True, vmem_limit_bytes=VMEM_LIMIT),
        name="wave_step",
    )(
        spectra, wind_growth.reshape(1, CELLS), wind_dir.reshape(1, CELLS), point_cell.reshape(1, CELLS),
        land_mask, shoaling, slope_x, slope_y,
    )
    out = out.reshape(NF, ND, 4, GX, 128)
    return jnp.transpose(out, (0, 1, 3, 2, 4)).reshape(NF, ND, GX, GY)


def solution(mesh):
    placed = (
        P(None, None, ("lon", "lat")),
        P(("lon", "lat")),
        P(("lon", "lat")),
        P(("lon", "lat")),
        P("lon", "lat"),
        P("lon", "lat"),
        P("lon", "lat"),
        P("lon", "lat"),
    )
    return jax.shard_map(
        on_device, mesh=mesh, in_specs=placed, out_specs=P(None, None, "lon", "lat"), check_vma=False
    )
```

time: 391 us -> 100 us (0.26)
  other arithmetic: 102 us -> 0 us
  Pallas kernels: 0 us -> 94.6 us
  local copies, waits for them, and re-layouts: 99 us -> 5.19 us
  waiting for transfers between devices: 80.8 us -> 0 us
  matrix products: 65.2 us -> 0 us
  starting transfers between devices: 39 us -> 0 us
    pallas_call x0 -> x1, Pallas kernels: none -> 94.6 us  [on_device(): pl.pallas_call(step_kernel, out_shape=jax.ShapeDtypeStruct((NF, ND, 8, 12...]
    dot_general x3 -> x0, matrix products: 65.2 us -> none  [the longest x2 63.7 us: route_rows(): jnp.dot(values, picker, precision=lax.Precision.HIGHEST, preferred_elemen...]
    ppermute x12 -> x0, waiting for transfers between devices: 52.3 us -> none  [the longest x6 34 us: with_halo(): lax.ppermute(tail, axis, [(i, (i + 1) % count) for i in range(count)])]
    mul x13 -> x0, other arithmetic: 33.8 us -> none  [the longest x2 22.7 us: on_device(): qx = cx_pad * padded]
    all_to_all x2 -> x0, waiting for transfers between devices: 28.5 us -> none  [the longest x1 28.5 us: on_device(): lax.all_to_all(outgoing, ('lon', 'lat'), split_axis=2, concat_axis=2, til...]
    unnamed x46 -> x1, local copies, waits for them, and re-layouts: 33 us -> 5.19 us
    add x6 -> x0, other arithmetic: 25.1 us -> none  [the longest x2 11.6 us: on_device(): jnp.maximum(qx[:, :, :-1, 1:-1], 0.0) + jnp.minimum(qx[:, :, 1:, 1:-1], 0.0)]
    all_to_all x2 -> x0, starting transfers between devices: 22.2 us -> none  [the longest x1 11.4 us: on_device(): lax.all_to_all(labels.reshape(1, 1, slots), ('lon', 'lat'), split_axis=2,...]
  transfers between devices with their start and end apart: 14 -> 0, of which waited for: 6 -> 0; matrix products, arithmetic and copies ran while one was open for 20% -> 0% of each run, Pallas kernels for 0% -> 0%
where the time goes in v2:
time: 100 us; the launch traced here: 99.8 us
  Pallas kernels  94.6 us (95%)
  local copies, waits for them, and re-layouts  5.19 us (5%)
    pallas_call x1, Pallas kernels, on_device(): pl.pallas_call(step_kernel, out_shape=jax.ShapeDtypeStruct((NF, ND, 8, 12...  94.6 us
    unnamed x1, local copies, waits for them, and re-layouts  5.19 us

profile of v2, /device:TPU:0, one launch (start us, length us, event | category | flops | bytes accessed | tf_op | source)
XLA Modules:
  0.0 99.8 jit_solution(14798323339837560800)
XLA Ops:
  0.0 94.6 %wave_step.1 = f32[25,36,8,128]{3,2,1,0:T(8,128)} custom-call(f32[25,36,1024]{2,1,0:T(8,128)} %spec_hbm.1, f32[1,1024]{1,0:T(1,128)} %bitcast.9, f32[1,1024]{1,0:T(1,128)} %bitcast.10, s32[1,1024]{1,0:T(1,128)} %bitcast.11, s32[2,512]{1,0:T(2,128)} %mask_ref.1, f32[2,512]{1,0:T(2,128)} %sh_ref.1, f32[2,512]{1,0:T(2,128)} %sx_ref.1, f32[2,512]{1,0:T(2,128)} %sy_ref.1), custom_call_target="tpu_custom_call" | custom-call | tf_op jit(solution)/shard_map/wave_step/pallas_call | solution.py:429
  94.6 5.2 %copy.11 = f32[25,36,2,512]{3,2,1,0:T(2,128)} copy(f32[25,36,2,512]{3,2,1,0:T(2,128)} %bitcast.8) | data formatting | bytes 7372800

commit v3 on v2

--- a/solution.py
+++ b/solution.py
@@ -1,3 +1,4 @@
+import functools
 import math
 
 import jax
@@ -94,24 +95,42 @@
     return v if k % 8 == 0 else pltpu.roll(v, k % 8, 0)
 
 
-def pack(lat, g, up_ref, dn_ref, yp_ref, ym_ref):
-    for k in range(PHALF):
-        up_ref[k] = jnp.where(lat.upper, g[CPLUS[k]], subs(g[CPLUS[k + PHALF]], 4))
-        dn_ref[k] = jnp.where(lat.upper, subs(g[CMINUS[k + PHALF]], 4), g[CMINUS[k]])
-    yp = jnp.zeros((8, 128), F32)
-    ym = jnp.zeros((8, 128), F32)
-    for k in range(18):
-        yp = jnp.where(lat.lane == k, lanes(g[SPLUS[k]], k + 1), yp)
-        ym = jnp.where(lat.lane == k, lanes(g[SMINUS[k]], k), ym)
-    yp_ref[...] = yp
-    ym_ref[...] = ym
-
-
-def substep(lat, field, sh, sea, turns, speed, up, dn, yp, ym):
+class Faces:
+    def __init__(self, lat, up_ref, dn_ref, yp_ref, ym_ref):
+        self.lat, self.up, self.dn, self.yp_ref, self.ym_ref = lat, up_ref, dn_ref, yp_ref, ym_ref
+        self.yp = jnp.zeros((8, 128), F32)
+        self.ym = jnp.zeros((8, 128), F32)
+
+    def put(self, d, g):
+        if d in CPLUS:
+            k = CPLUS.index(d)
+            if k < PHALF:
+                self.up[k, 4:8, :] = g[4:8, :]
+            else:
+                self.up[k - PHALF, 0:4, :] = g[4:8, :]
+        else:
+            k = CMINUS.index(d)
+            if k < PHALF:
+                self.dn[k, 0:4, :] = g[0:4, :]
+            else:
+                self.dn[k - PHALF, 4:8, :] = g[0:4, :]
+        if d in SPLUS:
+            k = SPLUS.index(d)
+            self.yp = jnp.where(self.lat.lane == k, lanes(g, k + 1), self.yp)
+        else:
+            k = SMINUS.index(d)
+            self.ym = jnp.where(self.lat.lane == k, lanes(g, k), self.ym)
+
+    def close(self):
+        self.yp_ref[...] = self.yp
+        self.ym_ref[...] = self.ym
+
+
+def substep(lat, field, sh, sea, turns, speed, up, dn, yp, ym, put):
     yp = subs(yp, 5)
     ym = subs(ym, 3)
-    half, pos, neg = [], [], []
-    for d in range(ND):
+
+    def moved(d):
         v = field(d)
         g = sh * v
         if d in CPLUS:
@@ -138,14 +157,15 @@
             gy = jnp.where(lat.last, lanes(ym, 127 - k), gy)
         h = v - (speed * abs(COS[d])) * (g - gx) - (speed * abs(SIN[d])) * (g - gy)
         qt = (speed * turns(d)) * h
-        half.append(h)
-        pos.append(jnp.maximum(qt, 0.0))
-        neg.append(jnp.minimum(qt, 0.0))
-    new = []
+        return h, jnp.maximum(qt, 0.0), jnp.minimum(qt, 0.0)
+
+    begin = moved(0)
+    end = moved(ND - 1)
+    west, here = end, begin
     for d in range(ND):
-        e, w = (d + 1) % ND, (d - 1) % ND
-        new.append((half[d] - (pos[d] + neg[e]) + (pos[w] + neg[d])) * sea)
-    return new
+        east = begin if d == ND - 1 else (end if d == ND - 2 else moved(d + 1))
+        put(d, (here[0] - (here[1] + east[2]) + (west[1] + here[2])) * sea)
+        west, here = here, east
 
 
 def fill_turns(turn_ref, sx_ref, sy_ref):
@@ -155,10 +175,11 @@
 
 
 def step_kernel(
-    spec_hbm, wg_ref, wd_ref, pc_ref, mask_ref, sh_ref, sx_ref, sy_ref, out_hbm,
+    spec_hbm, wg_hbm, wd_hbm, pc_hbm, mask_hbm, sh_hbm, sx_hbm, sy_hbm, out_hbm,
+    wg_ref, wd_ref, pc_ref, mask_ref, sh_ref, sx_ref, sy_ref,
     spec_ref, r_ref, v_ref, b_ref, sbuf, rbuf, ohs_ref, ohr_ref, field_ref, f1_ref, stage_ref, turn_ref,
     up_out, dn_out, yp_out, ym_out, up_in, dn_in, yp_in, ym_in, table,
-    spec_sem, send_sem, recv_sem, face_send, face_recv, out_sem,
+    small_sem, spec_sem, send_sem, recv_sem, face_send, face_recv, out_sem,
 ):
     lon = lax.axis_index("lon")
     x = lax.axis_index("lat")
@@ -171,25 +192,46 @@
     ynxt = (lon, lax.rem(x + 1, NLAT))
     yprv = (lon, lax.rem(x + NLAT - 1, NLAT))
 
+    barrier = pltpu.get_barrier_semaphore()
+    columns = [lax.rem(x + a, NLAT) for a in range(NLAT)]
+
+    def greet(k, carry):
+        row = lax.rem(lon + k, NLON)
+        for a in range(NLAT):
+            signal = functools.partial(
+                pl.semaphore_signal, barrier, 1, device_id=(row, columns[a]), device_id_type=MESH
+            )
+            if a == 0:
+                pl.when(k > 0)(signal)
+            else:
+                signal()
+        return carry
+
+    smalls = [
+        pltpu.make_async_copy(src, dst, small_sem.at[n])
+        for n, (src, dst) in enumerate(
+            (
+                (pc_hbm, pc_ref), (wd_hbm, wd_ref), (wg_hbm, wg_ref), (mask_hbm, mask_ref),
+                (sh_hbm, sh_ref), (sx_hbm, sx_ref), (sy_hbm, sy_ref),
+            )
+        )
+    ]
+    for cp in smalls:
+        cp.start()
     loads = [
         pltpu.make_async_copy(spec_hbm.at[pl.ds(5 * i, 5)], spec_ref.at[pl.ds(5 * i, 5)], spec_sem.at[i])
         for i in range(5)
     ]
     for cp in loads:
         cp.start()
-
-    barrier = pltpu.get_barrier_semaphore()
-
-    def greet(r, carry):
-        who = lax.rem(me + r, NDEV)
-        pl.semaphore_signal(barrier, 1, device_id=(lax.div(who, NLAT), lax.rem(who, NLAT)), device_id_type=MESH)
-        return carry
-
-    lax.fori_loop(1, NDEV, greet, 0)
+    lax.fori_loop(0, NLON, greet, 0, unroll=8)
+
     for f in range(NF):
         table[f] = jnp.float32(RATIO[f])
         table[32 + f] = jnp.float32(0.65 * 1.1 ** (-f))
 
+    for cp in smalls:
+        cp.wait()
     pc = pc_ref[...]
     valid = pc >= 0
     cell = jnp.maximum(pc, 0)
@@ -200,10 +242,16 @@
     owner = jnp.where(valid, owner, NDEV)
     own = (lax.broadcasted_iota(jnp.int32, (NDEV, CELLS), 0) == owner).astype(F32)
     own16 = own.astype(BF16)
-    ohs_ref[...] = (
-        lax.broadcasted_iota(jnp.int32, (CELLS, CELLS), 0) < lax.broadcasted_iota(jnp.int32, (CELLS, CELLS), 1)
+    upper = (
+        lax.broadcasted_iota(jnp.int32, (128, 128), 0) < lax.broadcasted_iota(jnp.int32, (128, 128), 1)
     ).astype(F32).astype(BF16)
-    before = nn_dot(own16, ohs_ref[...])
+    seen = jnp.zeros((NDEV, 1), F32)
+    blocks = []
+    for i in range(CELLS // 128):
+        part = own[:, 128 * i : 128 * (i + 1)]
+        blocks.append(nn_dot(part.astype(BF16), upper) + seen)
+        seen = seen + jnp.sum(part, axis=1, keepdims=True)
+    before = jnp.concatenate(blocks, axis=1)
     where = jnp.sum(before * own, axis=0, keepdims=True).astype(jnp.int32)
     target = jnp.where(valid, owner * CAP + where, CELLS)
     ohs_ref[...] = (lax.broadcasted_iota(jnp.int32, (CELLS, CELLS), 0) == target).astype(F32).astype(BF16)
@@ -293,13 +341,13 @@
     def prologue(t, carry):
         group(t)
 
-        @pl.when(t < 2)
+        @pl.when(t < 3)
         def _():
             push(tile(t), recv_sem.at[t])
 
         return carry
 
-    lax.fori_loop(0, 3, prologue, 0)
+    lax.fori_loop(0, 4, prologue, 0)
 
     sh = as_tile(sh_ref)
     sea = as_tile(mask_ref).astype(F32)
@@ -357,14 +405,14 @@
         for copy in faces(s, f):
             copy.wait_recv()
 
-    def wrap(s, f, g):
-        pack(lat, g, up_out.at[s, f], dn_out.at[s, f], yp_out.at[s, f], ym_out.at[s, f])
-
-    def propagate(s, f, get):
+    def outgoing(s, f):
+        return Faces(lat, up_out.at[s, f], dn_out.at[s, f], yp_out.at[s, f], ym_out.at[s, f])
+
+    def propagate(s, f, get, put):
         await_faces(s, f)
-        return substep(
+        substep(
             lat, get, sh, sea, lambda d: turn_ref[d], table[32 + f],
-            lambda k: up_in[s, f, k], lambda k: dn_in[s, f, k], yp_in[s, f] * low, ym_in[s, f] * high,
+            lambda k: up_in[s, f, k], lambda k: dn_in[s, f, k], yp_in[s, f] * low, ym_in[s, f] * high, put,
         )
 
     def over(lo, hi, fn):
@@ -374,20 +422,44 @@
 
         lax.fori_loop(lo, hi, body, 0)
 
+    def chain(lo, hi, fn, s):
+        def body(f, carry):
+            fn(f)
+
+            @pl.when(f > lo)
+            def _():
+                send(s, f - 1)
+
+            return carry
+
+        lax.fori_loop(lo, hi, body, 0)
+
+        @pl.when(hi > lo)
+        def _():
+            send(s, hi - 1)
+
     def start_face(f):
-        wrap(0, f, [sh * field_ref[row_dyn(f, d)] for d in range(ND)])
+        face = outgoing(0, f)
+        for d in range(ND):
+            face.put(d, sh * field_ref[row_dyn(f, d)])
+        face.close()
 
     def first(f):
-        new = propagate(0, f, lambda d: field_ref[row_dyn(f, d)])
-        for d in range(ND):
-            f1_ref[f, d] = new[d]
-        wrap(1, f, [sh * v for v in new])
+        face = outgoing(1, f)
+
+        def put(d, v):
+            f1_ref[f, d] = v
+            face.put(d, sh * v)
+
+        propagate(0, f, lambda d: field_ref[row_dyn(f, d)], put)
+        face.close()
 
     def second(f):
-        new = propagate(1, f, lambda d: f1_ref[f, d])
-        for d in range(ND):
-            stage_ref[f, d, pl.ds(0, 4, 2), :] = new[d][0:4, :]
-            stage_ref[f, d, pl.ds(1, 4, 2), :] = new[d][4:8, :]
+        def put(d, v):
+            stage_ref[f, d, pl.ds(0, 4, 2), :] = v[0:4, :]
+            stage_ref[f, d, pl.ds(1, 4, 2), :] = v[4:8, :]
+
+        propagate(1, f, lambda d: f1_ref[f, d], put)
 
     def emit(f):
         pltpu.make_async_copy(stage_ref.at[f], out_hbm.at[f], out_sem).start()
@@ -398,19 +470,17 @@
             arrive(tile(t), recv_sem.at[t])
             unplace(t)
 
-        over(whole(t), whole(t + 1), start_face)
-        over(whole(t), whole(t + 1), lambda f: send(0, f))
-
-        @pl.when(t + 2 < NT)
-        def _():
-            push(tile(t + 2), recv_sem.at[t + 2])
+        chain(whole(t), whole(t + 1), start_face, 0)
 
         @pl.when(t + 3 < NT)
         def _():
-            group(t + 3)
-
-        over(whole(t - 1), whole(t), first)
-        over(whole(t - 1), whole(t), lambda f: send(1, f))
+            push(tile(t + 3), recv_sem.at[t + 3])
+
+        @pl.when(t + 4 < NT)
+        def _():
+            group(t + 4)
+
+        chain(whole(t - 1), whole(t), first, 1)
         over(whole(t - 2), whole(t - 1), second)
         over(whole(t - 2), whole(t - 1), emit)
         return carry
@@ -424,14 +494,36 @@
     pltpu.make_async_copy(stage_ref, out_hbm, out_sem).wait()
 
 
+def emit_kernel(in_ref, out_ref, buf, in_sem, out_sem):
+    def part(i):
+        return pl.ds(5 * i, 5)
+
+    reads = [pltpu.make_async_copy(in_ref.at[part(i)], buf.at[part(i)], in_sem.at[i]) for i in range(5)]
+    writes = [pltpu.make_async_copy(buf.at[part(i)], out_ref.at[part(i)], out_sem.at[i]) for i in range(5)]
+    for cp in reads:
+        cp.start()
+    for read, write in zip(reads, writes):
+        read.wait()
+        write.start()
+    for cp in writes:
+        cp.wait()
+
+
 def on_device(spectra, wind_growth, wind_dir, point_cell, land_mask, shoaling, slope_x, slope_y):
     face = [(2, NF, PHALF, 8, 128), (2, NF, PHALF, 8, 128), (2, NF, 8, 128), (2, NF, 8, 128)]
     out = pl.pallas_call(
         step_kernel,
         out_shape=jax.ShapeDtypeStruct((NF, ND, 8, 128), F32),
-        in_specs=[pl.BlockSpec(memory_space=pl.ANY)] + [pl.BlockSpec(memory_space=pltpu.VMEM)] * 7,
+        in_specs=[pl.BlockSpec(memory_space=pl.ANY)] * 8,
         out_specs=pl.BlockSpec(memory_space=pl.ANY),
         scratch_shapes=[
+            pltpu.VMEM((1, CELLS), F32),
+            pltpu.VMEM((1, CELLS), F32),
+            pltpu.VMEM((1, CELLS), jnp.int32),
+            pltpu.VMEM((GX, GY), jnp.int32),
+            pltpu.VMEM((GX, GY), F32),
+            pltpu.VMEM((GX, GY), F32),
+            pltpu.VMEM((GX, GY), F32),
             pltpu.VMEM((NF, ND, CELLS), F32),
             pltpu.VMEM((40, CELLS), F32),
             pltpu.VMEM((904, CELLS), F32),
@@ -448,6 +540,7 @@
         + [pltpu.VMEM(s, F32) for s in face] * 2
         + [
             pltpu.SMEM((64,), F32),
+            pltpu.SemaphoreType.DMA((7,)),
             pltpu.SemaphoreType.DMA((5,)),
             pltpu.SemaphoreType.DMA,
             pltpu.SemaphoreType.DMA((NT + 1,)),
@@ -461,6 +554,19 @@
         spectra, wind_growth.reshape(1, CELLS), wind_dir.reshape(1, CELLS), point_cell.reshape(1, CELLS),
         land_mask, shoaling, slope_x, slope_y,
     )
+    out = pl.pallas_call(
+        emit_kernel,
+        out_shape=jax.ShapeDtypeStruct((NF, ND, 8, 128), F32),
+        in_specs=[pl.BlockSpec(memory_space=pl.ANY)],
+        out_specs=pl.BlockSpec(memory_space=pl.ANY),
+        scratch_shapes=[
+            pltpu.VMEM((NF, ND, 8, 128), F32),
+            pltpu.SemaphoreType.DMA((5,)),
+            pltpu.SemaphoreType.DMA((5,)),
+        ],
+        compiler_params=pltpu.CompilerParams(vmem_limit_bytes=VMEM_LIMIT),
+        name="emit",
+    )(out)
     out = out.reshape(NF, ND, 4, GX, 128)
     return jnp.transpose(out, (0, 1, 3, 2, 4)).reshape(NF, ND, GX, GY)
 

time: 100 us -> 85.4 us (0.85)
  Pallas kernels: 94.6 us -> 85.2 us
  local copies, waits for them, and re-layouts: 5.19 us -> 0 us
    pallas_call x1, Pallas kernels: 94.6 us -> 82.2 us  [on_device(): pl.pallas_call(step_kernel, out_shape=jax.ShapeDtypeStruct((NF, ND, 8, 12...]
    unnamed x1 -> x0, local copies, waits for them, and re-layouts: 5.19 us -> none
    pallas_call x0 -> x1, Pallas kernels: none -> 3.04 us  [on_device(): pl.pallas_call(emit_kernel, out_shape=jax.ShapeDtypeStruct((NF, ND, 8, 12...]
where the time goes in v3:
time: 85.4 us; the launch traced here: 85.2 us
  Pallas kernels  85.2 us (100%)
    pallas_call x1, Pallas kernels, on_device(): pl.pallas_call(step_kernel, out_shape=jax.ShapeDtypeStruct((NF, ND, 8, 12...  82.2 us
    pallas_call x1, Pallas kernels, on_device(): pl.pallas_call(emit_kernel, out_shape=jax.ShapeDtypeStruct((NF, ND, 8, 12...  3.04 us

profile of v3, /device:TPU:0, one launch (start us, length us, event | category | flops | bytes accessed | tf_op | source)
XLA Modules:
  0.0 85.2 jit_solution(5792610789021851136)
XLA Ops:
  0.0 82.2 %wave_step.1.in_ref = f32[25,36,8,128]{3,2,1,0:T(8,128)} custom-call(f32[25,36,1024]{2,1,0:T(8,128)} %spec_hbm.1, f32[1,1024]{1,0:T(1,128)} %bitcast.8, f32[1,1024]{1,0:T(1,128)} %bitcast.9, s32[1,1024]{1,0:T(1,128)} %bitcast.10, s32[2,512]{1,0:T(2,128)} %mask_hbm.1, f32[2,512]{1,0:T(2,128)} %sh_hbm.1, f32[2,512]{1,0:T(2,128)} %sx_hbm.1, f32[2,512]{1,0:T(2,128)} %sy_hbm.1), custom_call_target="tpu_custom_call" | custom-call | tf_op jit(solution)/shard_map/wave_step/pallas_call | solution.py:514
  82.2 3.0 %emit.1 = f32[25,36,8,128]{3,2,1,0:T(8,128)} custom-call(f32[25,36,8,128]{3,2,1,0:T(8,128)} %wave_step.1.in_ref), custom_call_target="tpu_custom_call" | custom-call | tf_op jit(solution)/shard_map/emit/pallas_call | solution.py:557

commit v4 on v3

--- a/solution.py
+++ b/solution.py
@@ -285,7 +285,7 @@
         b_ref[4 * s : 4 * s + 4, :] = last * here
         b_ref[4 * CAP + s : 4 * CAP + s + 1, :] = ident * here
     bh, bl = split(b_ref[...])
-    sbuf[:, 8 * NT, :] = nt_dot(own16, bh) + nt_dot(own16, bl)
+    sbuf[:, 8, :] = nt_dot(own16, bh) + nt_dot(own16, bl)
 
     def push(rows, sem):
         pltpu.make_async_copy(sbuf.at[me, rows], rbuf.at[me, rows], sem).start()
@@ -309,7 +309,9 @@
         lax.fori_loop(0, NDEV // 4, go, 0)
 
     def tile(t):
-        return pl.ds(pl.multiple_of(8 * t, 8), 8)
+        return pl.ds(pl.multiple_of(8 * (t + jnp.minimum(t, 1)), 8), 8)
+
+    front = pl.ds(0, 9)
 
     def arrive(rows, sem):
         pltpu.make_async_copy(rbuf.at[:, rows], rbuf.at[:, rows], sem).wait()
@@ -335,8 +337,9 @@
         res = both[:, :128] + both[:, 128:]
         sbuf[:, tile(t), :] = res.reshape(NDEV, CAP, 128)
 
+    group(jnp.int32(0))
     pl.semaphore_wait(barrier, NDEV - 1)
-    push(pl.ds(8 * NT, 1), recv_sem.at[NT])
+    push(front, recv_sem.at[0])
 
     def prologue(t, carry):
         group(t)
@@ -347,7 +350,7 @@
 
         return carry
 
-    lax.fori_loop(0, 4, prologue, 0)
+    lax.fori_loop(1, 4, prologue, 0)
 
     sh = as_tile(sh_ref)
     sea = as_tile(mask_ref).astype(F32)
@@ -356,8 +359,8 @@
     low = (x > 0).astype(F32)
     high = (x < NLAT - 1).astype(F32)
 
-    arrive(pl.ds(8 * NT, 1), recv_sem.at[NT])
-    tail = rbuf[:, 8 * NT, :]
+    arrive(front, recv_sem.at[0])
+    tail = rbuf[:, 8, :]
     ident = tail[:, 4 * CAP : 5 * CAP]
     spread = (
         lax.broadcasted_iota(jnp.int32, (CAP, CELLS), 1) % CAP == lax.broadcasted_iota(jnp.int32, (CAP, CELLS), 0)
@@ -465,9 +468,12 @@
         pltpu.make_async_copy(stage_ref.at[f], out_hbm.at[f], out_sem).start()
 
     def step(t, carry):
+        @pl.when((t > 0) & (t < NT))
+        def _():
+            arrive(tile(t), recv_sem.at[t])
+
         @pl.when(t < NT)
         def _():
-            arrive(tile(t), recv_sem.at[t])
             unplace(t)
 
         chain(whole(t), whole(t + 1), start_face, 0)
@@ -543,7 +549,7 @@
             pltpu.SemaphoreType.DMA((7,)),
             pltpu.SemaphoreType.DMA((5,)),
             pltpu.SemaphoreType.DMA,
-            pltpu.SemaphoreType.DMA((NT + 1,)),
+            pltpu.SemaphoreType.DMA((NT,)),
             pltpu.SemaphoreType.DMA((2, 4)),
             pltpu.SemaphoreType.DMA((2, 4, NF)),
             pltpu.SemaphoreType.DMA,

time: 85.4 us -> 83.8 us (0.981)
  Pallas kernels: 85.2 us -> 83.7 us
    pallas_call x1, Pallas kernels: 82.2 us -> 80.7 us  [on_device(): pl.pallas_call(step_kernel, out_shape=jax.ShapeDtypeStruct((NF, ND, 8, 12...]
where the time goes in v4:
time: 83.8 us; the launch traced here: 83.7 us
  Pallas kernels  83.7 us (100%)
    pallas_call x1, Pallas kernels, on_device(): pl.pallas_call(step_kernel, out_shape=jax.ShapeDtypeStruct((NF, ND, 8, 12...  80.7 us
    pallas_call x1, Pallas kernels, on_device(): pl.pallas_call(emit_kernel, out_shape=jax.ShapeDtypeStruct((NF, ND, 8, 12...  3.04 us

profile of v4, /device:TPU:0, one launch (start us, length us, event | category | flops | bytes accessed | tf_op | source)
XLA Modules:
  0.0 83.7 jit_solution(4831631472711886262)
XLA Ops:
  0.0 80.7 %wave_step.1.in_ref = f32[25,36,8,128]{3,2,1,0:T(8,128)} custom-call(f32[25,36,1024]{2,1,0:T(8,128)} %spec_hbm.1, f32[1,1024]{1,0:T(1,128)} %bitcast.8, f32[1,1024]{1,0:T(1,128)} %bitcast.9, s32[1,1024]{1,0:T(1,128)} %bitcast.10, s32[2,512]{1,0:T(2,128)} %mask_hbm.1, f32[2,512]{1,0:T(2,128)} %sh_hbm.1, f32[2,512]{1,0:T(2,128)} %sx_hbm.1, f32[2,512]{1,0:T(2,128)} %sy_hbm.1), custom_call_target="tpu_custom_call" | custom-call | tf_op jit(solution)/shard_map/wave_step/pallas_call | solution.py:520
  80.7 3.0 %emit.1 = f32[25,36,8,128]{3,2,1,0:T(8,128)} custom-call(f32[25,36,8,128]{3,2,1,0:T(8,128)} %wave_step.1.in_ref), custom_call_target="tpu_custom_call" | custom-call | tf_op jit(solution)/shard_map/emit/pallas_call | solution.py:563

commit v5 on v4

--- a/solution.py
+++ b/solution.py
@@ -224,7 +224,7 @@
     ]
     for cp in loads:
         cp.start()
-    lax.fori_loop(0, NLON, greet, 0, unroll=8)
+    lax.fori_loop(0, NLON, greet, 0, unroll=32)
 
     for f in range(NF):
         table[f] = jnp.float32(RATIO[f])

time: 83.8 us -> 83.7 us (level)
  no operation moved by 1% of the time
where the time goes in v5:
time: 83.7 us; the launch traced here: 83.6 us
  Pallas kernels  83.6 us (100%)
    pallas_call x1, Pallas kernels, on_device(): pl.pallas_call(step_kernel, out_shape=jax.ShapeDtypeStruct((NF, ND, 8, 12...  80.5 us
    pallas_call x1, Pallas kernels, on_device(): pl.pallas_call(emit_kernel, out_shape=jax.ShapeDtypeStruct((NF, ND, 8, 12...  3.04 us

profile of v5, /device:TPU:0, one launch (start us, length us, event | category | flops | bytes accessed | tf_op | source)
XLA Modules:
  0.0 83.6 jit_solution(2693785898025117289)
XLA Ops:
  0.0 80.5 %wave_step.1.in_ref = f32[25,36,8,128]{3,2,1,0:T(8,128)} custom-call(f32[25,36,1024]{2,1,0:T(8,128)} %spec_hbm.1, f32[1,1024]{1,0:T(1,128)} %bitcast.8, f32[1,1024]{1,0:T(1,128)} %bitcast.9, s32[1,1024]{1,0:T(1,128)} %bitcast.10, s32[2,512]{1,0:T(2,128)} %mask_hbm.1, f32[2,512]{1,0:T(2,128)} %sh_hbm.1, f32[2,512]{1,0:T(2,128)} %sx_hbm.1, f32[2,512]{1,0:T(2,128)} %sy_hbm.1), custom_call_target="tpu_custom_call" | custom-call | tf_op jit(solution)/shard_map/wave_step/pallas_call | solution.py:520
  80.5 3.0 %emit.1 = f32[25,36,8,128]{3,2,1,0:T(8,128)} custom-call(f32[25,36,8,128]{3,2,1,0:T(8,128)} %wave_step.1.in_ref), custom_call_target="tpu_custom_call" | custom-call | tf_op jit(solution)/shard_map/emit/pallas_call | solution.py:563
